TPU v7x, 512 devices: a whole 4x4x16 slice. The times are simulated.
512 devices in a mesh: dx: 8 (over x, core), dy: 2 (over y_hi), band: 32 (over y_lo, z).
Axes of the slice: x: 4, y: 4 (y_hi: 2, y_lo: 2; y = y_hi * 2 + y_lo), z: 16, core: 2. Of those that a mesh axis runs over, the one named last changes fastest.
Arguments:
- orbitals: bfloat16 [128, 96, 8192], P('dx', 'dy', 'band'), may hold values from -6 to 6
- rotation: bfloat16 [2048, 2048], P('band'), may hold values from -0.125 to 0.125
- potential: float32 [4, 128, 96], P(None, 'dx', 'dy'), may hold values from -3 to 1
Outputs:
- rotated: bfloat16 [128, 96, 8192], P('dx', 'dy', 'band')
- applied: bfloat16 [128, 96, 8192], P('dx', 'dy', 'band')
All inputs are finite; a program needn't handle non-finite values.
Results may differ from a plain program's by a relative error of at most 0.0049.
Values may be sent and summed in bfloat16 or wider, within the bound.
No kernel may reach another device: no remote copies, remote signals or barrier semaphores. Data moves between devices by JAX's collectives and lax.ppermute only.
A program may use at most 64 MiB of HBM per device.

v0:
```python
import jax
import jax.numpy as jnp
from jax import lax
from jax.sharding import PartitionSpec as P

stencil_weights = (-205.0 / 72.0, 8.0 / 5.0, -1.0 / 5.0, 8.0 / 315.0, -1.0 / 560.0)


def with_halo(cells, sides, width):
    for axis, dim in sides:
        count = lax.axis_size(axis)
        ends = count - 1
        head = lax.slice_in_dim(cells, 0, width, axis=dim)
        tail = lax.slice_in_dim(cells, cells.shape[dim] - width, cells.shape[dim], axis=dim)
        cells = jnp.concatenate(
            [
                lax.ppermute(tail, axis, [(i, (i + 1) % count) for i in range(ends)]),
                cells,
                lax.ppermute(head, axis, [((i + 1) % count, i) for i in range(ends)]),
            ],
            axis=dim,
        )
    return cells


def on_device(orbitals, rotation, potential):
    planes = potential.shape[0]
    cells_x, cells_y, merged = orbitals.shape
    local_bands = merged // planes
    points = cells_x * cells_y
    by_plane = jnp.transpose(orbitals.reshape(points, local_bands, planes), (0, 2, 1))
    flat = by_plane.reshape(points * planes, local_bands)
    summed = lax.dot_general(
        lax.all_gather(flat, "band", axis=1, tiled=True),
        rotation,
        (((1,), (1,)), ((), ())),
        preferred_element_type=jnp.float32,
    )
    mixed_local = summed.astype(jnp.bfloat16).reshape(points, planes, local_bands)
    rotated = jnp.transpose(mixed_local, (0, 2, 1)).reshape(cells_x, cells_y, merged)
    padded = with_halo(rotated, (("dx", 0), ("dy", 1)), 4)
    x_padded = padded[:, 4 : 4 + cells_y]
    y_padded = padded[4 : 4 + cells_x, :]
    center = rotated.astype(jnp.float32)
    x_wide = x_padded.astype(jnp.float32)
    y_wide = y_padded.astype(jnp.float32)
    plane_index = lax.broadcasted_iota(jnp.int32, (1, 1, merged), 2) % planes
    laplace = 3.0 * stencil_weights[0] * center
    for distance in range(1, 5):
        weight = stencil_weights[distance]
        tail = jnp.zeros((cells_x, cells_y, distance), jnp.float32)
        upper = jnp.concatenate([center[:, :, distance:], tail], axis=2)
        lower = jnp.concatenate([tail, center[:, :, : merged - distance]], axis=2)
        upper = jnp.where(plane_index + distance < planes, upper, 0.0)
        lower = jnp.where(plane_index - distance >= 0, lower, 0.0)
        along_z = upper + lower
        along_x = (
            x_wide[4 + distance : 4 + distance + cells_x]
            + x_wide[4 - distance : 4 - distance + cells_x]
        )
        along_y = (
            y_wide[:, 4 + distance : 4 + distance + cells_y]
            + y_wide[:, 4 - distance : 4 - distance + cells_y]
        )
        laplace = laplace + weight * (along_z + along_x + along_y)
    field = jnp.tile(jnp.transpose(potential, (1, 2, 0)), (1, 1, local_bands))
    applied = -0.5 * laplace + field * center
    return (rotated, applied.astype(jnp.bfloat16))


def solution(mesh):
    return jax.shard_map(
        on_device,
        mesh=mesh,
        in_specs=(P("dx", "dy", "band"), P("band", None), P(None, "dx", "dy")),
        out_specs=(P("dx", "dy", "band"), P("dx", "dy", "band")),
        check_vma=False,
    )
```

profile of v0, /device:TPU:1, one launch (start us, length us, event | category | flops | bytes accessed | tf_op | source)
XLA Modules:
  0.0 250.6 jit_solution(14161555101341242040)
XLA Ops:
  7.2 0.0 copy-start
  7.2 0.0 all-gather.2.cloned.1.call-start
  7.2 2.0 copy.35
  9.2 1.2 reshape.76
  10.4 0.6 copy.36
  11.0 1.0 copy.37
  12.0 0.0 all-gather.2.cloned.1.call-update
  12.1 0.6 add_compare_fusion.2
  12.7 0.6 add_compare_fusion.4
  13.3 0.6 add_compare_fusion.6
  13.9 155.9 %all-gather.2.cloned.1.call-done = bf16[3072,2048]{0,1:T(8,128)(2,1)} async-done(((bf16[3072,64]{0,1:T(8,128)(2,1)}), bf16[3072,2048]{0,1:T(8,128)(2,1)}) %all-gather.2.cloned.1.call-update) | async-done | bytes 12582928 | tf_op jit(solution)/shard_map/all_gather | solution.py:34
  169.7 0.0 copy-done
  169.7 6.9 %convolution_convert_fusion = bf16[3072,64]{0,1:T(8,128)(2,1)S(1)} fusion(bf16[64,2048]{1,0:T(8,128)(2,1)S(1)} %copy-done, bf16[3072,2048]{0,1:T(8,128)(2,1)} %all-gather.2.cloned.1.call-done), kind=kOutput, calls=%fused_computation | convolution fusion | flops 805502976 | bytes 13238272 | tf_op jit(solution)/shard_map/dot_general | solution.py:33
  176.6 0.4 copy.38
  177.0 0.6 copy.39
  177.6 0.9 fusion.26
  178.5 1.0 reshape.79
  179.4 2.4 fusion.23
  181.8 1.7 fusion.22
  183.5 1.1 copy.41
  184.6 0.9 slice.98
  185.5 6.2 %collective-permute-start.1 = (bf16[4,48,256]{1,0,2:T(4,128)(2,1)}, bf16[4,48,256]{1,0,2:T(4,128)(2,1)}, u32[]{:S(2)}, u32[]{:S(2)}) collective-permute-start(bf16[4,48,256]{1,0,2:T(4,128)(2,1)} %slice.98), channel_id=1, source_target_pairs={{64,0},{128,64},{192,128},{256,192},{320,256},{384,320},{448,384},... | collective-permute-start | bytes 294920 | tf_op jit(solution)/shard_map/ppermute | solution.py:19
  191.7 1.2 copy.40
  192.9 0.9 slice.96
  193.8 3.0 %collective-permute-start = (bf16[4,48,256]{1,0,2:T(4,128)(2,1)}, bf16[4,48,256]{1,0,2:T(4,128)(2,1)S(1)}, u32[]{:S(2)}, u32[]{:S(2)}) collective-permute-start(bf16[4,48,256]{1,0,2:T(4,128)(2,1)} %slice.96), channel_id=1, source_target_pairs={{0,64},{64,128},{128,192},{192,256},{256,320},{320,384},{384,448},... | collective-permute-start | bytes 294920 | tf_op jit(solution)/shard_map/ppermute | solution.py:17
  196.8 2.4 fusion.24
  199.2 0.0 collective-permute-done.1
  199.2 1.2 collective-permute-done
  200.4 0.0 copy-start.3
  200.4 3.6 %fusion.20 = (f32[24,48,256]{1,0,2:T(8,128)}, bf16[24,48,256]{1,0,2:T(8,128)(2,1)S(1)}) fusion(bf16[4,48,256]{1,0,2:T(4,128)(2,1)} %collective-permute-done.1, bf16[16,48,256]{1,0,2:T(8,128)(2,1)S(1)} %reshape.79, bf16[4,48,256]{1,0,2:T(4,128)(2,1)S(1)} %collective-permute-done), kind=kLoop, calls=%fused_computation.44 | loop fusion | flops 2064384 | bytes 2359296 | tf_op jit(solution)/shard_map/convert_element_type | solution.py:45
  204.0 0.0 copy-done.3
  204.0 2.3 fusion.21
  206.3 2.2 copy.43
  208.5 1.3 collective-permute-start.3
  209.8 2.2 copy.42
  212.0 6.1 %collective-permute-start.2 = (bf16[24,4,256]{2,0,1:T(8,128)(2,1)S(1)}, bf16[24,4,256]{2,0,1:T(8,128)(2,1)}, u32[]{:S(2)}, u32[]{:S(2)}) collective-permute-start(bf16[24,4,256]{2,0,1:T(8,128)(2,1)S(1)} %copy.42), channel_id=1, source_target_pairs={{0,32},{1,33},{2,34},{3,35},{4,36},{5,37},{6,38},{7,39},{8,40},{9,... | collective-permute-start | bytes 147464 | tf_op jit(solution)/shard_map/ppermute | solution.py:17
  218.1 2.2 fusion.25
  220.3 1.6 copy.46
  221.9 0.0 collective-permute-done.3
  222.0 1.8 copy.45
  223.7 0.0 collective-permute-done.2
  223.7 2.4 copy.44
  226.2 0.0 copy-start.1
  226.2 0.0 copy-start.2
  226.2 0.0 copy-start.4
  226.2 0.0 copy-start.5
  226.2 0.0 copy-start.6
  226.2 0.0 copy-start.7
  226.2 0.0 copy-start.8
  226.2 0.0 copy-start.9
  226.2 0.0 copy-start.10
  226.2 3.7 %fusion.19 = f32[16,56,256]{1,0,2:T(8,128)S(1)} fusion(bf16[24,4,256]{1,0,2:T(8,128)(2,1)} %copy.45, bf16[24,4,256]{1,0,2:T(8,128)(2,1)} %copy.44, bf16[4,48,256]{1,0,2:T(4,128)(2,1)} %collective-permute-done.1, bf16[16,48,256]{1,0,2:T(8,128)(2,1)S(1)} %reshape.79, bf16[4,48,256]{1,0,2:T(4,128)(2,1)} %copy-done.3), kind=kLoop, calls=%fused_computation.31 | loop fusion | flops 2293760 | bytes 1605632 | tf_op jit(solution)/shard_map/convert_element_type | solution.py:46
  229.9 0.0 copy-done.1
  229.9 0.0 copy-done.2
  230.0 0.0 copy-done.4
  230.0 0.0 copy-done.5
  230.0 0.0 copy-done.6
  230.0 0.0 copy-done.7
  230.0 0.0 copy-done.8
  230.0 0.0 copy-done.9
  230.0 0.0 copy-done.10
  230.0 11.0 %fusion.5 = bf16[16,48,256]{1,0,2:T(8,128)(2,1)} fusion(f32[16,56,256]{1,0,2:T(8,128)S(1)} %fusion.19, f32[24,48,256]{1,0,2:T(8,128)S(1)} %copy-done.1, f32[16,48,252]{1,0,2:T(8,128)} %get-tuple-element.19, f32[16,48,252]{1,0,2:T(8,128)} %get-tuple-element.18, f32[16,48,253]{1,0,2:T(8,128)} %get-tuple-element.17, f32[16,48,253]{1,0,2:T(8,128)} %get-tuple-element.16, ...), kind=kLoop, calls=%fused_computation.7 | loop fusion | flops 8257536 | bytes 19613696 | tf_op jit(solution)/shard_map/convert_element_type | solution.py:68
  241.0 2.7 %copy.47 = bf16[16,48,256]{2,1,0:T(8,128)(2,1)} copy(bf16[16,48,256]{1,0,2:T(8,128)(2,1)} %fusion.5) | data formatting | bytes 786432
  (1 shorter events, 0.0 us)
Async XLA Ops:
  7.2 162.6 %copy-start = (bf16[64,2048]{1,0:T(8,128)(2,1)S(1)}, bf16[64,2048]{1,0:T(8,128)(2,1)}, u32[]{:S(2)}) copy-start(bf16[64,2048]{1,0:T(8,128)(2,1)} %param.4) | copy-start | bytes 786436
  7.2 162.6 %all-gather.2.cloned.1.call-start = ((), (), s32[]{:S(2)}) async-start(), calls=%async_computation | async-start | bytes 12976128 | tf_op jit(solution)/shard_map/all_gather | solution.py:34
  185.5 13.7 %collective-permute-start.1 = (bf16[4,48,256]{1,0,2:T(4,128)(2,1)}, bf16[4,48,256]{1,0,2:T(4,128)(2,1)}, u32[]{:S(2)}, u32[]{:S(2)}) collective-permute-start(bf16[4,48,256]{1,0,2:T(4,128)(2,1)} %slice.98), channel_id=1, source_target_pairs={{64,0},{128,64},{192,128},{256,192},{320,256},{384,320},{448,384},... | collective-permute-start | bytes 294920 | tf_op jit(solution)/shard_map/ppermute | solution.py:19
  193.8 6.6 %collective-permute-start = (bf16[4,48,256]{1,0,2:T(4,128)(2,1)}, bf16[4,48,256]{1,0,2:T(4,128)(2,1)S(1)}, u32[]{:S(2)}, u32[]{:S(2)}) collective-permute-start(bf16[4,48,256]{1,0,2:T(4,128)(2,1)} %slice.96), channel_id=1, source_target_pairs={{0,64},{64,128},{128,192},{192,256},{256,320},{320,384},{384,448},... | collective-permute-start | bytes 294920 | tf_op jit(solution)/shard_map/ppermute | solution.py:17
  200.4 3.6 %copy-start.3 = (bf16[4,48,256]{1,0,2:T(4,128)(2,1)}, bf16[4,48,256]{1,0,2:T(4,128)(2,1)S(1)}, u32[]{:S(2)}) copy-start(bf16[4,48,256]{1,0,2:T(4,128)(2,1)S(1)} %collective-permute-done) | copy-start | bytes 294916
  208.5 13.4 %collective-permute-start.3 = (bf16[24,4,256]{2,0,1:T(8,128)(2,1)S(1)}, bf16[24,4,256]{2,0,1:T(8,128)(2,1)S(1)}, u32[]{:S(2)}, u32[]{:S(2)}) collective-permute-start(bf16[24,4,256]{2,0,1:T(8,128)(2,1)S(1)} %copy.43), channel_id=1, source_target_pairs={{32,0},{33,1},{34,2},{35,3},{36,4},{37,5},{38,6},{39,7},{40,8},{41... | collective-permute-start | bytes 147464 | tf_op jit(solution)/shard_map/ppermute | solution.py:19
  212.0 11.7 %collective-permute-start.2 = (bf16[24,4,256]{2,0,1:T(8,128)(2,1)S(1)}, bf16[24,4,256]{2,0,1:T(8,128)(2,1)}, u32[]{:S(2)}, u32[]{:S(2)}) collective-permute-start(bf16[24,4,256]{2,0,1:T(8,128)(2,1)S(1)} %copy.42), channel_id=1, source_target_pairs={{0,32},{1,33},{2,34},{3,35},{4,36},{5,37},{6,38},{7,39},{8,40},{9,... | collective-permute-start | bytes 147464 | tf_op jit(solution)/shard_map/ppermute | solution.py:17
  226.2 3.8 %copy-start.1 = (f32[24,48,256]{1,0,2:T(8,128)S(1)}, f32[24,48,256]{1,0,2:T(8,128)}, u32[]{:S(2)}) copy-start(f32[24,48,256]{1,0,2:T(8,128)} %get-tuple-element.8) | copy-start | bytes 3538948
  226.2 3.8 %copy-start.2 = (f32[16,48,255]{1,0,2:T(8,128)S(1)}, f32[16,48,255]{1,0,2:T(8,128)}, u32[]{:S(2)}) copy-start(f32[16,48,255]{1,0,2:T(8,128)} %get-tuple-element.13) | copy-start | bytes 2350084
  226.2 3.8 %copy-start.4 = (f32[4,16,48]{2,1,0:T(8,128)S(1)}, f32[4,16,48]{2,1,0:T(8,128)}, u32[]{:S(2)}) copy-start(f32[4,16,48]{2,1,0:T(8,128)} %param.5) | copy-start | bytes 36868
  226.2 3.8 %copy-start.5 = (pred[256]{0:T(512)(128)(4,1)S(1)}, pred[256]{0:T(512)(128)(4,1)}, u32[]{:S(2)}) copy-start(pred[256]{0:T(512)(128)(4,1)} %get-tuple-element.24) | copy-start | bytes 772
  226.2 3.8 %copy-start.6 = (pred[256]{0:T(512)(128)(4,1)S(1)}, pred[256]{0:T(512)(128)(4,1)}, u32[]{:S(2)}) copy-start(pred[256]{0:T(512)(128)(4,1)} %get-tuple-element.25) | copy-start | bytes 772
  226.2 3.8 %copy-start.7 = (pred[256]{0:T(512)(128)(4,1)S(1)}, pred[256]{0:T(512)(128)(4,1)}, u32[]{:S(2)}) copy-start(pred[256]{0:T(512)(128)(4,1)} %get-tuple-element.26) | copy-start | bytes 772
  226.2 3.8 %copy-start.8 = (pred[256]{0:T(512)(128)(4,1)S(1)}, pred[256]{0:T(512)(128)(4,1)}, u32[]{:S(2)}) copy-start(pred[256]{0:T(512)(128)(4,1)} %get-tuple-element.27) | copy-start | bytes 772
  226.2 3.8 %copy-start.9 = (pred[256]{0:T(512)(128)(4,1)S(1)}, pred[256]{0:T(512)(128)(4,1)}, u32[]{:S(2)}) copy-start(pred[256]{0:T(512)(128)(4,1)} %get-tuple-element.28) | copy-start | bytes 772
  226.2 3.8 %copy-start.10 = (pred[256]{0:T(512)(128)(4,1)S(1)}, pred[256]{0:T(512)(128)(4,1)}, u32[]{:S(2)}) copy-start(pred[256]{0:T(512)(128)(4,1)} %get-tuple-element.29) | copy-start | bytes 772
Sparse Core Ops, SparseCore 0:
  12.2 157.5 all-gather.1
where the time goes:
time: 252 us; the launch traced here: 251 us
  waiting for transfers between devices  157 us (62%)
  local copies, waits for them, and re-layouts  35.6 us (14%)
  other arithmetic  20.1 us (8%)
  starting transfers between devices  16.6 us (7%)
  between operations  14.3 us (6%)
  matrix products  6.87 us (3%)
    all_gather x1, waiting for transfers between devices, on_device(): lax.all_gather(flat, 'band', axis=1, tiled=True)  156 us
    convert_element_type x1, other arithmetic, on_device(): return (rotated, applied.astype(jnp.bfloat16))  11 us
    ppermute x2, starting transfers between devices, with_halo(): lax.ppermute(tail, axis, [(i, (i + 1) % count) for i in range(ends)])  9.09 us
    slice x4, local copies, waits for them, and re-layouts, on_device(): upper = jnp.concatenate([center[:, :, distance:], tail], axis=2)  8.63 us
    ppermute x2, starting transfers between devices, with_halo(): lax.ppermute(head, axis, [((i + 1) % count, i) for i in range(ends)])  7.49 us
    slice x5, local copies, waits for them, and re-layouts, with_halo(): lax.slice_in_dim(cells, cells.shape[dim] - width, cells.shape[dim], axis=...  7.46 us
    dot_general x1, matrix products, on_device(): lax.dot_general(lax.all_gather(flat, 'band', axis=1, tiled=True), rotatio...  6.87 us
    unnamed x25, local copies, waits for them, and re-layouts  6.35 us
  transfers between devices with their start and end apart: 5, of which 2 were waited for; matrix products, arithmetic and copies ran while one was open for 6% of the time, Pallas kernels for 0%

commit v1 on v0

v1 whole, which is shorter than its diff:
```python
import functools

import jax
import jax.numpy as jnp
from jax import lax
from jax.experimental import pallas as pl
from jax.experimental.pallas import tpu as pltpu
from jax.sharding import PartitionSpec as P

stencil_weights = (-205.0 / 72.0, 8.0 / 5.0, -1.0 / 5.0, 8.0 / 315.0, -1.0 / 560.0)
PLANES = 4
VMEM = pl.BlockSpec(memory_space=pltpu.VMEM)
SMEM = pl.BlockSpec(memory_space=pltpu.SMEM)


def expand_kernel(rows_ref, out_ref):
    bands, width = rows_ref.shape
    spread = width * PLANES
    lane = lax.broadcasted_iota(jnp.int32, (spread, width), 0) // PLANES
    pick = (lane == lax.broadcasted_iota(jnp.int32, (spread, width), 1)).astype(jnp.bfloat16)
    tall = lax.dot_general(
        pick, rows_ref[...], (((1,), (1,)), ((), ())), preferred_element_type=jnp.float32
    ).astype(jnp.bfloat16)
    wide = bands * PLANES
    source = lax.broadcasted_iota(jnp.int32, (bands, wide), 0)
    target = lax.broadcasted_iota(jnp.int32, (bands, wide), 1) // PLANES
    full = jnp.dot(tall, (source == target).astype(jnp.bfloat16), preferred_element_type=jnp.float32)
    plane_in = lax.broadcasted_iota(jnp.int32, (spread, wide), 0) % PLANES
    plane_out = lax.broadcasted_iota(jnp.int32, (spread, wide), 1) % PLANES
    full = jnp.where(plane_in == plane_out, full, 0.0).astype(jnp.bfloat16)
    out_ref[...] = full.reshape(out_ref.shape)


def expand(rows):
    bands, total = rows.shape
    width = 128
    half = width * PLANES // 2
    return pl.pallas_call(
        expand_kernel,
        grid=(total // width,),
        in_specs=[pl.BlockSpec((bands, width), lambda i: (0, i))],
        out_specs=pl.BlockSpec((2, half, bands * PLANES), lambda i: (i, 0, 0)),
        out_shape=jax.ShapeDtypeStruct((2 * total // width, half, bands * PLANES), jnp.bfloat16),
        cost_estimate=pl.CostEstimate(flops=3 * 10**9, bytes_accessed=9 * 2**20, transcendentals=0),
        name="expand",
    )(rows)


def rotate_kernel(where_ref, psi_ref, near_ref, far_ref, keep_ref, send_ref, total_ref):
    step = pl.program_id(0)
    count = psi_ref.shape[0]
    part = None
    for k in range(count):
        for side, weights in ((0, near_ref), (1, far_ref)):
            term = jnp.dot(psi_ref[k, side], weights[0, k], preferred_element_type=jnp.float32)
            part = term if part is None else part + term

    @pl.when(step == 0)
    def _():
        total_ref[...] = part

    @pl.when(step > 0)
    def _():
        total_ref[...] += part

    @pl.when(step == pl.num_programs(0) - 1)
    def _():
        lanes = keep_ref.shape[1]
        keep_ref[...] = total_ref[:, :lanes].astype(jnp.bfloat16)
        send_ref[...] = total_ref[:, lanes:].astype(jnp.bfloat16)


def rotate(side, psi, weights):
    ring, _, points, lanes = psi.shape
    together = min(4, ring)
    block = (1, together, lanes, 2 * lanes)
    out = jax.ShapeDtypeStruct((points, lanes), jnp.bfloat16)
    return pl.pallas_call(
        rotate_kernel,
        grid_spec=pltpu.PrefetchScalarGridSpec(
            num_scalar_prefetch=1,
            grid=(ring // together,),
            in_specs=[
                pl.BlockSpec((together, 2, points, lanes), lambda i, s: (i, 0, 0, 0)),
                pl.BlockSpec(block, lambda i, s: (s[0], i, 0, 0)),
                pl.BlockSpec(block, lambda i, s: (1 - s[0], i, 0, 0)),
            ],
            out_specs=[pl.BlockSpec((points, lanes), lambda i, s: (0, 0))] * 2,
            scratch_shapes=[pltpu.VMEM((points, 2 * lanes), jnp.float32)],
        ),
        out_shape=[out, out],
        name="rotate",
    )(side, psi, weights, weights)


def edges_kernel(place_ref, keep_ref, got_ref, rotated_ref, low_ref, high_ref, side_ref):
    half = keep_ref.shape[0]
    mine = place_ref[0]
    rotated_ref[pl.ds(half * mine, half)] = keep_ref[...]
    rotated_ref[pl.ds(half * (1 - mine), half)] = got_ref[...]
    low_ref[...] = rotated_ref[:4]
    high_ref[...] = rotated_ref[2 * half - 4 :]
    cells_y = rotated_ref.shape[1]

    @pl.when(place_ref[1] == 0)
    def _():
        side_ref[...] = rotated_ref[:, cells_y - 4 :]

    @pl.when(place_ref[1] != 0)
    def _():
        side_ref[...] = rotated_ref[:, :4]


def edges(place, keep, got):
    half, cells_y, lanes = keep.shape
    shapes = [(2 * half, cells_y, lanes), (4, cells_y, lanes), (4, cells_y, lanes), (2 * half, 4, lanes)]
    return pl.pallas_call(
        edges_kernel,
        in_specs=[SMEM, VMEM, VMEM],
        out_specs=[VMEM] * 4,
        out_shape=[jax.ShapeDtypeStruct(s, jnp.bfloat16) for s in shapes],
        name="edges",
    )(place, keep, got)


def stencil_kernel(place_ref, rotated_ref, low_ref, high_ref, side_ref, field_ref, out_ref, pad_ref):
    cells_x, cells_y, lanes = rotated_ref.shape
    rows = slice(8, 8 + cells_y)
    pad_ref[4 : 4 + cells_x, rows] = rotated_ref[...].astype(jnp.float32)
    pad_ref[0:4, rows] = low_ref[...].astype(jnp.float32)
    pad_ref[4 + cells_x :, rows] = high_ref[...].astype(jnp.float32)
    beside = side_ref[...].astype(jnp.float32)
    first = place_ref[1] == 0
    pad_ref[4 : 4 + cells_x, 4:8] = jnp.where(first, 0.0, beside)
    pad_ref[4 : 4 + cells_x, 8 + cells_y : 12 + cells_y] = jnp.where(first, beside, 0.0)
    plane = lax.broadcasted_iota(jnp.int32, (cells_y, lanes), 1) % PLANES

    def row(x, carry):
        center = pad_ref[x + 4, rows]
        laplace = 3.0 * stencil_weights[0] * center
        for d in range(1, 5):
            total = pad_ref[x + 4 + d, rows] + pad_ref[x + 4 - d, rows]
            total += pad_ref[x + 4, 8 + d : 8 + d + cells_y] + pad_ref[x + 4, 8 - d : 8 - d + cells_y]
            if d < PLANES:
                total += jnp.where(plane + d < PLANES, pltpu.roll(center, lanes - d, 1), 0.0)
                total += jnp.where(plane >= d, pltpu.roll(center, d, 1), 0.0)
            laplace += stencil_weights[d] * total
        out_ref[x] = (field_ref[x] * center - 0.5 * laplace).astype(jnp.bfloat16)
        return carry

    lax.fori_loop(0, cells_x, row, 0)


def stencil(place, rotated, low, high, side, field):
    cells_x, cells_y, lanes = rotated.shape
    return pl.pallas_call(
        stencil_kernel,
        in_specs=[SMEM] + [VMEM] * 5,
        out_specs=VMEM,
        out_shape=jax.ShapeDtypeStruct(rotated.shape, jnp.bfloat16),
        scratch_shapes=[pltpu.VMEM((cells_x + 8, cells_y + 16, lanes), jnp.float32)],
        name="stencil",
    )(place, rotated, low, high, side, field)


def on_device(orbitals, rotation, potential):
    cells_x, cells_y, lanes = orbitals.shape
    half = cells_x // 2
    columns = lax.axis_size("band")
    ring = columns // 2
    mine = lax.axis_index("band") // ring
    across = [(i, (i + ring) % columns) for i in range(columns)]
    place = jnp.stack([mine, lax.axis_index("dy")]).astype(jnp.int32)

    sent = lax.dynamic_slice_in_dim(orbitals, half * (1 - mine), half, 0)
    kept = lax.dynamic_slice_in_dim(orbitals, half * mine, half, 0)
    came = lax.ppermute(sent, "band", across)
    rows = jnp.concatenate([rotation, lax.ppermute(rotation, "band", across)], axis=0)
    both = jnp.stack([kept, came]).reshape(1, 2, half * cells_y, lanes)
    groups = [list(range(ring)), list(range(ring, columns))]
    psi = lax.all_gather(both, "band", axis=0, tiled=True, axis_index_groups=groups)
    weights = expand(rows)
    weights = weights.reshape(2, ring, lanes, 2 * lanes)
    keep, send = rotate(place[:1], psi, weights)
    got = lax.ppermute(send, "band", across)
    shape = (half, cells_y, lanes)
    rotated, low, high, side = edges(place, keep.reshape(shape), got.reshape(shape))
    ends = lax.axis_size("dx") - 1
    above = lax.ppermute(high, "dx", [(i, i + 1) for i in range(ends)])
    below = lax.ppermute(low, "dx", [(i + 1, i) for i in range(ends)])
    beside = lax.ppermute(side, "dy", [(0, 1), (1, 0)])
    field = jnp.tile(jnp.transpose(potential, (1, 2, 0)), (1, 1, lanes // PLANES))
    applied = stencil(place, rotated, above, below, beside, field)
    return rotated, applied


def solution(mesh):
    return jax.shard_map(
        on_device,
        mesh=mesh,
        in_specs=(P("dx", "dy", "band"), P("band", None), P(None, "dx", "dy")),
        out_specs=(P("dx", "dy", "band"), P("dx", "dy", "band")),
        check_vma=False,
    )
```

time: 252 us -> 154 us (0.61)
  waiting for transfers between devices: 157 us -> 79.5 us
  local copies, waits for them, and re-layouts: 35.6 us -> 4.57 us
  Pallas kernels: 0 us -> 27.2 us
  other arithmetic: 20.1 us -> 3.24 us
  starting transfers between devices: 16.6 us -> 24 us
  matrix products: 6.87 us -> 0 us
    all_gather x1, waiting for transfers between devices: 156 us -> 68.1 us  [on_device(): lax.all_gather(both, 'band', axis=0, tiled=True, axis_index_groups=groups)]
    pallas_call x0 -> x4, Pallas kernels: none -> 27.2 us  [the longest x1 12.3 us: expand(): pl.pallas_call(expand_kernel, grid=(total // width,), in_specs=[pl.BlockS...]
    slice x12 -> x0, local copies, waits for them, and re-layouts: 20.3 us -> none  [the longest x4 8.63 us: on_device(): upper = jnp.concatenate([center[:, :, distance:], tail], axis=2)]
    convert_element_type x3 -> x0, other arithmetic: 18.3 us -> none  [the longest x1 11 us: on_device(): return (rotated, applied.astype(jnp.bfloat16))]
    ppermute x4 -> x6, waiting for transfers between devices: 1.22 us -> 11.4 us  [the longest x1 5.27 us: on_device(): lax.ppermute(rotation, 'band', across)]
    ppermute x4 -> x6, starting transfers between devices: 16.6 us -> 24 us  [the longest x1 6.63 us: on_device(): above = lax.ppermute(high, 'dx', [(i, i + 1) for i in range(ends)])]
    dot_general x1 -> x0, matrix products: 6.87 us -> none  [on_device(): lax.dot_general(lax.all_gather(flat, 'band', axis=1, tiled=True), rotatio...]
    unnamed x25 -> x10, local copies, waits for them, and re-layouts: 6.35 us -> 1.36 us
  transfers between devices with their start and end apart: 5 -> 7, of which waited for: 2 -> 4; matrix products, arithmetic and copies ran while one was open for 6% -> 3% of each run, Pallas kernels for 0% -> 8%
where the time goes in v1:
time: 154 us; the launch traced here: 153 us
  waiting for transfers between devices  79.5 us (52%)
  Pallas kernels  27.2 us (18%)
  starting transfers between devices  24 us (16%)
  between operations  14.2 us (9%)
  local copies, waits for them, and re-layouts  4.57 us (3%)
  other arithmetic  3.24 us (2%)
    all_gather x1, waiting for transfers between devices, on_device(): lax.all_gather(both, 'band', axis=0, tiled=True, axis_index_groups=groups)  68.1 us
    pallas_call x1, Pallas kernels, expand(): pl.pallas_call(expand_kernel, grid=(total // width,), in_specs=[pl.BlockS...  12.3 us
    pallas_call x1, Pallas kernels, rotate(): pl.pallas_call(rotate_kernel, grid_spec=pltpu.PrefetchScalarGridSpec(num_...  8.23 us
    ppermute x1, starting transfers between devices, on_device(): above = lax.ppermute(high, 'dx', [(i, i + 1) for i in range(ends)])  6.63 us
    ppermute x1, waiting for transfers between devices, on_device(): lax.ppermute(rotation, 'band', across)  5.27 us
    ppermute x1, starting transfers between devices, on_device(): beside = lax.ppermute(side, 'dy', [(0, 1), (1, 0)])  5.17 us
    pallas_call x1, Pallas kernels, stencil(): pl.pallas_call(stencil_kernel, in_specs=[SMEM] + [VMEM] * 5, out_specs=VM...  4.81 us
    ppermute x1, starting transfers between devices, on_device(): came = lax.ppermute(sent, 'band', across)  4.02 us
  transfers between devices with their start and end apart: 7, of which 4 were waited for; matrix products, arithmetic and copies ran while one was open for 3% of the time, Pallas kernels for 8%

profile of v1, /device:TPU:1, one launch (start us, length us, event | category | flops | bytes accessed | tf_op | source)
XLA Modules:
  0.0 152.7 jit_solution(15600821984851350344)
XLA Ops:
  7.2 0.0 all-gather.2.cloned.1.call-start
  7.2 1.1 constant_dynamic-slice_fusion.1
  8.3 4.0 %collective-permute-start = (bf16[8,48,256]{2,1,0:T(8,128)(2,1)S(1)}, bf16[8,48,256]{2,1,0:T(8,128)(2,1)S(1)}, u32[]{:S(2)}, u32[]{:S(2)}) collective-permute-start(bf16[8,48,256]{2,1,0:T(8,128)(2,1)S(1)} %get-tuple-element.15), channel_id=1, source_target_pairs={{0,16},{1,17},{2,18},{3,19},{4,20},{5,21},{6,22},{7,23},{8,24},{9,... | collective-permute-start | bytes 589832 | tf_op jit(solution)/shard_map/ppermute | solution.py:177
  12.3 3.0 %collective-permute-done = bf16[8,48,256]{2,1,0:T(8,128)(2,1)S(1)} collective-permute-done((bf16[8,48,256]{2,1,0:T(8,128)(2,1)S(1)}, bf16[8,48,256]{2,1,0:T(8,128)(2,1)S(1)}, u32[]{:S(2)}, u32[]{:S(2)}) %collective-permute-start) | collective-permute-done | bytes 196640 | tf_op jit(solution)/shard_map/ppermute | solution.py:177
  15.4 0.8 pad_maximum_fusion.1
  16.1 0.0 all-gather.2.cloned.1.call-update
  16.2 3.4 %collective-permute-start.1 = (bf16[64,2048]{1,0:T(8,128)(2,1)}, bf16[64,2048]{1,0:T(8,128)(2,1)S(1)}, u32[]{:S(2)}, u32[]{:S(2)}) collective-permute-start(bf16[64,2048]{1,0:T(8,128)(2,1)} %param.4), channel_id=1, source_target_pairs={{0,16},{1,17},{2,18},{3,19},{4,20},{5,21},{6,22},{7,23},{8,24},{9,... | collective-permute-start | bytes 786440 | tf_op jit(solution)/shard_map/ppermute | solution.py:178
  19.5 5.3 %collective-permute-done.1 = bf16[64,2048]{1,0:T(8,128)(2,1)S(1)} collective-permute-done((bf16[64,2048]{1,0:T(8,128)(2,1)}, bf16[64,2048]{1,0:T(8,128)(2,1)S(1)}, u32[]{:S(2)}, u32[]{:S(2)}) %collective-permute-start.1) | collective-permute-done | bytes 262176 | tf_op jit(solution)/shard_map/ppermute | solution.py:178
  24.8 1.8 %pad_maximum_fusion.rows_ref = bf16[128,2048]{1,0:T(8,128)(2,1)} fusion(bf16[64,2048]{1,0:T(8,128)(2,1)S(1)} %collective-permute-done.1, bf16[64,2048]{1,0:T(8,128)(2,1)} %param.4), kind=kLoop, calls=%fused_computation | loop fusion | flops 1048576 | bytes 1048576 | tf_op jit(solution)/shard_map/concatenate | solution.py:178
  26.6 12.3 %expand.1 = bf16[32,256,512]{2,1,0:T(8,128)(2,1)} custom-call(bf16[128,2048]{1,0:T(8,128)(2,1)} %pad_maximum_fusion.rows_ref), custom_call_target="tpu_custom_call" | custom-call | flops 3000000000 | bytes 9437184 | tf_op jit(solution)/shard_map/expand/pallas_call | solution.py:38
  38.9 68.1 %all-gather.2.cloned.1.call-done.psi_ref = bf16[16,2,384,256]{3,2,1,0:T(8,128)(2,1)} async-done(((bf16[1,2,384,256]{3,2,1,0:T(8,128)(2,1)}), bf16[16,2,384,256]{3,2,1,0:T(8,128)(2,1)}) %all-gather.2.cloned.1.call-update) | async-done | bytes 6291472 | tf_op jit(solution)/shard_map/all_gather | solution.py:181
  106.9 0.0 copy-start.3
  106.9 8.2 %rotate.1 = (bf16[384,256]{1,0:T(8,128)(2,1)}, bf16[384,256]{1,0:T(8,128)(2,1)}) custom-call(s32[1]{0:T(128)} %bitcast.where_ref, bf16[16,2,384,256]{3,2,1,0:T(8,128)(2,1)} %all-gather.2.cloned.1.call-done.psi_ref, bf16[2,16,256,512]{3,2,1,0:T(8,128)(2,1)} %bitcast.9, bf16[2,16,256,512]{3,2,1,0:T(8,128)(2,1)} %bitcast.10), custom_call_target="tpu_custom_call" | custom-call | tf_op jit(solution)/shard_map/rotate/pallas_call | solution.py:78
  115.2 2.9 %collective-permute-start.2 = (bf16[384,256]{1,0:T(8,128)(2,1)}, bf16[384,256]{1,0:T(8,128)(2,1)S(1)}, u32[]{:S(2)}, u32[]{:S(2)}) collective-permute-start(bf16[384,256]{1,0:T(8,128)(2,1)} %get-tuple-element.9), channel_id=1, source_target_pairs={{0,16},{1,17},{2,18},{3,19},{4,20},{5,21},{6,22},{7,23},{8,24},{9,... | collective-permute-start | bytes 589832 | tf_op jit(solution)/shard_map/ppermute | solution.py:185
  118.1 0.7 pad_add_fusion.place_ref
  118.7 3.1 %collective-permute-done.2 = bf16[384,256]{1,0:T(8,128)(2,1)S(1)} collective-permute-done((bf16[384,256]{1,0:T(8,128)(2,1)}, bf16[384,256]{1,0:T(8,128)(2,1)S(1)}, u32[]{:S(2)}, u32[]{:S(2)}) %collective-permute-start.2) | collective-permute-done | bytes 196640 | tf_op jit(solution)/shard_map/ppermute | solution.py:185
  121.8 0.0 copy-start
  121.8 0.7 copy-done
  122.5 1.9 %edges.1 = (bf16[16,48,256]{2,1,0:T(8,128)(2,1)}, bf16[4,48,256]{2,1,0:T(8,128)(2,1)}, bf16[4,48,256]{2,1,0:T(8,128)(2,1)}, bf16[16,4,256]{2,1,0:T(4,128)(2,1)}) custom-call(s32[2]{0:T(128)} %pad_add_fusion.place_ref, bf16[8,48,256]{2,1,0:T(8,128)(2,1)} %bitcast.13, bf16[8,48,256]{2,1,0:T(8,128)(2,1)} %bitcast.14), custom_call_target="tpu_custom_call" | custom-call | tf_op jit(solution)/shard_map/edges/pallas_call | solution.py:117
  124.4 6.6 %collective-permute-start.3 = (bf16[4,48,256]{2,1,0:T(8,128)(2,1)}, bf16[4,48,256]{2,1,0:T(8,128)(2,1)S(1)}, u32[]{:S(2)}, u32[]{:S(2)}) collective-permute-start(bf16[4,48,256]{2,1,0:T(8,128)(2,1)} %get-tuple-element.11), channel_id=1, source_target_pairs={{0,64},{64,128},{128,192},{192,256},{256,320},{320,384},{384,448},... | collective-permute-start | bytes 294920 | tf_op jit(solution)/shard_map/ppermute | solution.py:189
  131.0 1.9 %collective-permute-start.4 = (bf16[4,48,256]{2,1,0:T(8,128)(2,1)}, bf16[4,48,256]{2,1,0:T(8,128)(2,1)S(1)}, u32[]{:S(2)}, u32[]{:S(2)}) collective-permute-start(bf16[4,48,256]{2,1,0:T(8,128)(2,1)} %get-tuple-element.12), channel_id=1, source_target_pairs={{64,0},{128,64},{192,128},{256,192},{320,256},{384,320},{448,384},... | collective-permute-start | bytes 294920 | tf_op jit(solution)/shard_map/ppermute | solution.py:190
  132.9 5.2 %collective-permute-start.5 = (bf16[16,4,256]{2,1,0:T(4,128)(2,1)}, bf16[16,4,256]{2,1,0:T(4,128)(2,1)S(1)}, u32[]{:S(2)}, u32[]{:S(2)}) collective-permute-start(bf16[16,4,256]{2,1,0:T(4,128)(2,1)} %get-tuple-element.13), channel_id=1, source_target_pairs={{0,32},{32,0},{1,33},{33,1},{2,34},{34,2},{3,35},{35,3},{4,36},{36... | collective-permute-start | bytes 98312 | tf_op jit(solution)/shard_map/ppermute | solution.py:191
  138.1 0.0 copy-done.3
  138.1 0.2 tile.4
  138.4 1.9 %copy.7.field_ref = f32[16,48,256]{2,1,0:T(8,128)} copy(f32[16,48,256]{1,0,2:T(8,128)S(1)} %bitcast.11) | data formatting | bytes 1572864 | tf_op jit(solution)/shard_map/tile | solution.py:192
  140.3 0.0 collective-permute-done.5.side_ref
  140.3 0.0 copy-start.4
  140.3 0.0 collective-permute-done.3.low_ref
  140.3 0.0 copy-start.1
  140.3 0.0 collective-permute-done.4.high_ref
  140.3 0.0 copy-start.2
  140.3 0.6 copy-done.4
  140.9 0.0 copy-done.1
  140.9 0.1 copy-done.2
  141.0 4.8 %stencil.1 = bf16[16,48,256]{2,1,0:T(8,128)(2,1)} custom-call(s32[2]{0:T(128)} %pad_add_fusion.place_ref, bf16[16,48,256]{2,1,0:T(8,128)(2,1)} %get-tuple-element.6.rotated_ref, bf16[4,48,256]{2,1,0:T(8,128)(2,1)} %copy-done.1, bf16[4,48,256]{2,1,0:T(8,128)(2,1)} %copy-done.2, bf16[16,4,256]{2,1,0:T(4,128)(2,1)} %copy-done.4, f32[16,48,256]{2,1,0:T(8,128)} %copy.7.field_ref), custom_call_target="tpu_custom_call" | custom-call | tf_op jit(solution)/shard_map/stencil/pallas_call | solution.py:156
Async XLA Ops:
  7.2 99.8 %all-gather.2.cloned.1.call-start = ((), (), s32[]{:S(2)}) async-start(), calls=%async_computation | async-start | bytes 6684672 | tf_op jit(solution)/shard_map/all_gather | solution.py:181
  8.3 7.1 %collective-permute-start = (bf16[8,48,256]{2,1,0:T(8,128)(2,1)S(1)}, bf16[8,48,256]{2,1,0:T(8,128)(2,1)S(1)}, u32[]{:S(2)}, u32[]{:S(2)}) collective-permute-start(bf16[8,48,256]{2,1,0:T(8,128)(2,1)S(1)} %get-tuple-element.15), channel_id=1, source_target_pairs={{0,16},{1,17},{2,18},{3,19},{4,20},{5,21},{6,22},{7,23},{8,24},{9,... | collective-permute-start | bytes 589832 | tf_op jit(solution)/shard_map/ppermute | solution.py:177
  16.2 8.6 %collective-permute-start.1 = (bf16[64,2048]{1,0:T(8,128)(2,1)}, bf16[64,2048]{1,0:T(8,128)(2,1)S(1)}, u32[]{:S(2)}, u32[]{:S(2)}) collective-permute-start(bf16[64,2048]{1,0:T(8,128)(2,1)} %param.4), channel_id=1, source_target_pairs={{0,16},{1,17},{2,18},{3,19},{4,20},{5,21},{6,22},{7,23},{8,24},{9,... | collective-permute-start | bytes 786440 | tf_op jit(solution)/shard_map/ppermute | solution.py:178
  106.9 31.2 %copy-start.3 = (f32[4,16,48]{2,1,0:T(8,128)S(1)}, f32[4,16,48]{2,1,0:T(8,128)}, u32[]{:S(2)}) copy-start(f32[4,16,48]{2,1,0:T(8,128)} %param.5) | copy-start | bytes 36868
  115.2 6.6 %collective-permute-start.2 = (bf16[384,256]{1,0:T(8,128)(2,1)}, bf16[384,256]{1,0:T(8,128)(2,1)S(1)}, u32[]{:S(2)}, u32[]{:S(2)}) collective-permute-start(bf16[384,256]{1,0:T(8,128)(2,1)} %get-tuple-element.9), channel_id=1, source_target_pairs={{0,16},{1,17},{2,18},{3,19},{4,20},{5,21},{6,22},{7,23},{8,24},{9,... | collective-permute-start | bytes 589832 | tf_op jit(solution)/shard_map/ppermute | solution.py:185
  121.8 0.7 copy-start
  124.4 15.9 %collective-permute-start.3 = (bf16[4,48,256]{2,1,0:T(8,128)(2,1)}, bf16[4,48,256]{2,1,0:T(8,128)(2,1)S(1)}, u32[]{:S(2)}, u32[]{:S(2)}) collective-permute-start(bf16[4,48,256]{2,1,0:T(8,128)(2,1)} %get-tuple-element.11), channel_id=1, source_target_pairs={{0,64},{64,128},{128,192},{192,256},{256,320},{320,384},{384,448},... | collective-permute-start | bytes 294920 | tf_op jit(solution)/shard_map/ppermute | solution.py:189
  131.0 9.3 %collective-permute-start.4 = (bf16[4,48,256]{2,1,0:T(8,128)(2,1)}, bf16[4,48,256]{2,1,0:T(8,128)(2,1)S(1)}, u32[]{:S(2)}, u32[]{:S(2)}) collective-permute-start(bf16[4,48,256]{2,1,0:T(8,128)(2,1)} %get-tuple-element.12), channel_id=1, source_target_pairs={{64,0},{128,64},{192,128},{256,192},{320,256},{384,320},{448,384},... | collective-permute-start | bytes 294920 | tf_op jit(solution)/shard_map/ppermute | solution.py:190
  132.9 7.4 %collective-permute-start.5 = (bf16[16,4,256]{2,1,0:T(4,128)(2,1)}, bf16[16,4,256]{2,1,0:T(4,128)(2,1)S(1)}, u32[]{:S(2)}, u32[]{:S(2)}) collective-permute-start(bf16[16,4,256]{2,1,0:T(4,128)(2,1)} %get-tuple-element.13), channel_id=1, source_target_pairs={{0,32},{32,0},{1,33},{33,1},{2,34},{34,2},{3,35},{35,3},{4,36},{36... | collective-permute-start | bytes 98312 | tf_op jit(solution)/shard_map/ppermute | solution.py:191
  140.3 0.6 copy-start.4
  140.3 0.6 copy-start.1
  140.3 0.7 copy-start.2
Sparse Core Ops, SparseCore 0:
  16.3 90.6 all-gather.1

commit v2 on v0

v2 whole, which is shorter than its diff:
```python
import functools

import jax
import jax.numpy as jnp
from jax import lax
from jax.experimental import pallas as pl
from jax.experimental.pallas import tpu as pltpu
from jax.sharding import PartitionSpec as P

stencil_weights = (-205.0 / 72.0, 8.0 / 5.0, -1.0 / 5.0, 8.0 / 315.0, -1.0 / 560.0)
PLANES = 4
VMEM = pl.BlockSpec(memory_space=pltpu.VMEM)
SMEM = pl.BlockSpec(memory_space=pltpu.SMEM)


def rotate_kernel(first, last, begin, count, *refs):
    place_ref, order_ref, rows_ref = refs[:3]
    blocks = refs[3 : 3 + count]
    refs = refs[3 + count :]
    if not first:
        before_ref, refs = refs[0], refs[1:]
    if first:
        levels_ref, refs = refs[0], refs[1:]
    bands = rows_ref.shape[0]
    lanes = blocks[0].shape[1]
    wide = bands * PLANES
    i = lax.broadcasted_iota(jnp.int32, (bands, wide), 0)
    spread = (i == lax.broadcasted_iota(jnp.int32, (bands, wide), 1) >> 2).astype(jnp.bfloat16)
    row = lax.broadcasted_iota(jnp.int32, (lanes, 128), 0) >> 2
    column = lax.broadcasted_iota(jnp.int32, (lanes, 128), 1)
    i = lax.broadcasted_iota(jnp.int32, (lanes, wide), 0)
    same = ((i ^ lax.broadcasted_iota(jnp.int32, (lanes, wide), 1)) & (PLANES - 1)) == 0
    total = None if first else before_ref[...]
    for k in range(count):
        block = order_ref[begin + k]
        start = pl.multiple_of((block >> 1) * 128, 128)
        pick = (row + (block & 1) * (lanes // PLANES) == column).astype(jnp.bfloat16)
        tall = lax.dot_general(
            pick,
            rows_ref[:, pl.ds(start, 128)],
            (((1,), (1,)), ((), ())),
            preferred_element_type=jnp.float32,
        ).astype(jnp.bfloat16)
        full = jnp.dot(tall, spread, preferred_element_type=jnp.float32)
        weights = jnp.where(same, full, 0.0).astype(jnp.bfloat16)
        term = jnp.dot(blocks[k][...], weights, preferred_element_type=jnp.float32)
        total = term if total is None else total + term
    if first:
        out_ref, field_ref = refs
        planes, cells_x, cells_y = levels_ref.shape
        q = lax.broadcasted_iota(jnp.int32, (planes, lanes), 1) & (PLANES - 1)
        cover = (q == lax.broadcasted_iota(jnp.int32, (planes, lanes), 0)).astype(jnp.float32)
        for x in range(cells_x):
            field_ref[x] = lax.dot_general(
                levels_ref[:, x],
                cover,
                (((0,), (0,)), ((), ())),
                precision=lax.Precision.HIGHEST,
                preferred_element_type=jnp.float32,
            )
    elif last:
        keep_ref, send_ref, keep_x_ref, send_x_ref, keep_y_ref, send_y_ref = refs
        near = total[:, :lanes].astype(jnp.bfloat16)
        far = total[:, lanes:].astype(jnp.bfloat16)
        keep_ref[...] = near
        send_ref[...] = far
        tall = keep_x_ref.shape[0]
        edge = pl.multiple_of(place_ref[0] * tall, tall)
        keep_x_ref[...] = keep_ref[pl.ds(edge, tall)]
        send_x_ref[...] = send_ref[pl.ds(edge, tall)]
        cells_x = keep_y_ref.shape[0]
        near = near.reshape(cells_x, -1, lanes)
        far = far.reshape(cells_x, -1, lanes)
        cells_y = near.shape[1]

        @pl.when(place_ref[1] == 0)
        def _():
            keep_y_ref[...] = near[:, cells_y - 4 :]
            send_y_ref[...] = far[:, cells_y - 4 :]

        @pl.when(place_ref[1] != 0)
        def _():
            keep_y_ref[...] = near[:, :4]
            send_y_ref[...] = far[:, :4]

        return
    else:
        (out_ref,) = refs
    out_ref[...] = total


def rotate(place, order, rows, begin, blocks, before, levels, cells, last):
    first = before is None
    points, lanes = blocks[0].shape
    total = jax.ShapeDtypeStruct((points, 2 * lanes), jnp.float32)
    args = [place, order, rows, *blocks]
    alias = {}
    if first:
        args.append(levels)
        out = [total, jax.ShapeDtypeStruct((*levels.shape[1:], lanes), jnp.float32)]
    else:
        args.append(before)
        if last:
            cells_x, cells_y = cells
            half = jax.ShapeDtypeStruct((points, lanes), jnp.bfloat16)
            x_edge = jax.ShapeDtypeStruct((4 * cells_y, lanes), jnp.bfloat16)
            y_edge = jax.ShapeDtypeStruct((cells_x, 4, lanes), jnp.bfloat16)
            out = [half, half, x_edge, x_edge, y_edge, y_edge]
        else:
            alias = {len(args) - 1: 0}
            out = [total]
    return pl.pallas_call(
        functools.partial(rotate_kernel, first, last, begin, len(blocks)),
        in_specs=[SMEM, SMEM] + [VMEM] * (len(args) - 2),
        out_specs=[VMEM] * len(out),
        out_shape=out,
        input_output_aliases=alias,
        cost_estimate=pl.CostEstimate(
            flops=2 * 10**8 * len(blocks), bytes_accessed=3 * 2**20, transcendentals=0
        ),
        name="rotate",
    )(*args)


def stencil_kernel(
    place_ref, keep_ref, got_ref, keep_x_ref, send_x_ref, keep_y_ref, send_y_ref, field_ref,
    rotated_ref, out_ref, pad_ref,
):
    cells_x, cells_y, lanes = rotated_ref.shape
    half = cells_x // 2
    rows = slice(8, 8 + cells_y)
    mine = place_ref[0]
    near, far = half * mine, half * (1 - mine)
    rotated_ref[pl.ds(near, half)] = keep_ref[...]
    rotated_ref[pl.ds(far, half)] = got_ref[...]
    pad_ref[pl.ds(4 + near, half), rows] = keep_ref[...].astype(jnp.float32)
    pad_ref[pl.ds(4 + far, half), rows] = got_ref[...].astype(jnp.float32)
    reach = cells_x + 4
    pad_ref[pl.ds(reach * (1 - mine), 4), rows] = keep_x_ref[...].astype(jnp.float32)
    pad_ref[pl.ds(reach * mine, 4), rows] = send_x_ref[...].astype(jnp.float32)
    keep_y = keep_y_ref[...].astype(jnp.float32)
    send_y = send_y_ref[...].astype(jnp.float32)
    first = place_ref[1] == 0
    above = slice(8 + cells_y, 12 + cells_y)
    pad_ref[pl.ds(4 + near, half), 4:8] = jnp.where(first, 0.0, keep_y)
    pad_ref[pl.ds(4 + far, half), 4:8] = jnp.where(first, 0.0, send_y)
    pad_ref[pl.ds(4 + near, half), above] = jnp.where(first, keep_y, 0.0)
    pad_ref[pl.ds(4 + far, half), above] = jnp.where(first, send_y, 0.0)
    plane = lax.broadcasted_iota(jnp.int32, (cells_y, lanes), 1) & (PLANES - 1)

    def row(x, carry):
        center = pad_ref[x + 4, rows]
        laplace = 3.0 * stencil_weights[0] * center
        for d in range(1, 5):
            total = pad_ref[x + 4 + d, rows] + pad_ref[x + 4 - d, rows]
            total += pad_ref[x + 4, 8 + d : 8 + d + cells_y] + pad_ref[x + 4, 8 - d : 8 - d + cells_y]
            if d < PLANES:
                total += jnp.where(plane + d < PLANES, pltpu.roll(center, lanes - d, 1), 0.0)
                total += jnp.where(plane >= d, pltpu.roll(center, d, 1), 0.0)
            laplace += stencil_weights[d] * total
        out_ref[x] = (field_ref[x] * center - 0.5 * laplace).astype(jnp.bfloat16)
        return carry

    lax.fori_loop(0, cells_x, row, 0)


def stencil(place, *arrays):
    half, cells_y, lanes = arrays[0].shape
    cells_x = 2 * half
    out = jax.ShapeDtypeStruct((cells_x, cells_y, lanes), jnp.bfloat16)
    return pl.pallas_call(
        stencil_kernel,
        in_specs=[SMEM] + [VMEM] * len(arrays),
        out_specs=[VMEM] * 2,
        out_shape=[out, out],
        scratch_shapes=[pltpu.VMEM((cells_x + 8, cells_y + 16, lanes), jnp.float32)],
        name="stencil",
    )(place, *arrays)


def on_device(orbitals, rotation, potential):
    cells_x, cells_y, lanes = orbitals.shape
    half = cells_x // 2
    points = half * cells_y
    columns = lax.axis_size("band")
    ring = columns // 2
    index = lax.axis_index("band")
    mine, z = index // ring, index % ring
    place = jnp.stack([mine, lax.axis_index("dy")]).astype(jnp.int32)
    across = [(i, (i + ring) % columns) for i in range(columns)]
    hops = {
        step: [(i, i // ring * ring + (i + step) % ring) for i in range(columns)]
        for step in (1, -1)
    }

    sent = lax.dynamic_slice_in_dim(orbitals, half * (1 - mine), half, 0)
    kept = lax.dynamic_slice_in_dim(orbitals, half * mine, half, 0)
    came = lax.ppermute(sent.reshape(points, lanes), "band", across)
    rows = jnp.concatenate([rotation, lax.ppermute(rotation, "band", across)], axis=0)

    blocks = [{0: kept.reshape(points, lanes)}, {0: came}]
    far = ring // 2
    for distance in range(1, far + 1):
        for side in (0, 1):
            for step in (1, -1):
                if distance < far or (step == 1) == (side == 0):
                    held = blocks[side][step * (distance - 1)]
                    blocks[side][step * distance] = lax.ppermute(held, "band", hops[step])
    steps = []
    for distance in range(far + 1):
        for side in (0, 1):
            steps += [(side, d) for d in sorted({distance, -distance}) if d in blocks[side]]
    sides = jnp.asarray([s for s, _ in steps], jnp.int32)
    offsets = jnp.asarray([d for _, d in steps], jnp.int32)
    order = ((mine + sides) % 2 * ring + (z - offsets) % ring).astype(jnp.int32)

    total, field, begin = None, None, 0
    tail = min(4, len(steps) // 2)
    cuts = [*range(8, len(steps) - tail, 8), len(steps) - tail, len(steps)]
    for end in cuts:
        group = [blocks[side][d] for side, d in steps[begin:end]]
        last = end == len(steps)
        out = rotate(place, order, rows, begin, group, total, potential, (half, cells_y), last)
        if total is None:
            total, field = out
        elif not last:
            (total,) = out
        begin = end
    keep, send, keep_x, send_x, keep_y, send_y = out

    ends = lax.axis_size("dx") - 1
    near, cross = [], []
    for x in range(ends):
        for i in range(ring):
            low, high = i, ring + i
            near += [(x * columns + high, (x + 1) * columns + high)]
            near += [((x + 1) * columns + low, x * columns + low)]
            cross += [(x * columns + high, (x + 1) * columns + low)]
            cross += [((x + 1) * columns + low, x * columns + high)]
    got = lax.ppermute(send, "band", across)
    keep_x = lax.ppermute(keep_x, ("dx", "band"), near)
    send_x = lax.ppermute(send_x, ("dx", "band"), cross)
    keep_y = lax.ppermute(keep_y, "dy", [(0, 1), (1, 0)])
    turn = [
        (y * columns + i, (1 - y) * columns + (i + ring) % columns)
        for y in range(2)
        for i in range(columns)
    ]
    send_y = lax.ppermute(send_y, ("dy", "band"), turn)
    shape = (half, cells_y, lanes)
    edge = (4, cells_y, lanes)
    rotated, applied = stencil(
        place, keep.reshape(shape), got.reshape(shape), keep_x.reshape(edge), send_x.reshape(edge),
        keep_y, send_y, field,
    )
    return rotated, applied


def solution(mesh):
    return jax.shard_map(
        on_device,
        mesh=mesh,
        in_specs=(P("dx", "dy", "band"), P("band", None), P(None, "dx", "dy")),
        out_specs=(P("dx", "dy", "band"), P("dx", "dy", "band")),
        check_vma=False,
    )
```

time: 252 us -> 173 us (0.69)
  waiting for transfers between devices: 157 us -> 2.01 us
  starting transfers between devices: 16.6 us -> 128 us
  Pallas kernels: 0 us -> 33.5 us
  local copies, waits for them, and re-layouts: 35.6 us -> 3.98 us
  other arithmetic: 20.1 us -> 1.14 us
  between operations: 14.3 us -> 1.58 us
  matrix products: 6.87 us -> 0 us
    all_gather x1 -> x0, waiting for transfers between devices: 156 us -> none  [on_device(): lax.all_gather(flat, 'band', axis=1, tiled=True)]
    ppermute x4 -> x37, starting transfers between devices: 16.6 us -> 128 us  [the longest x30 95.6 us: on_device(): blocks[side][step * distance] = lax.ppermute(held, 'band', hops[step])]
    pallas_call x0 -> x6, Pallas kernels: none -> 33.5 us  [the longest x5 28.5 us: rotate(): pl.pallas_call(functools.partial(rotate_kernel, first, last, begin, len(b...]
    slice x12 -> x0, local copies, waits for them, and re-layouts: 20.3 us -> none  [the longest x4 8.63 us: on_device(): upper = jnp.concatenate([center[:, :, distance:], tail], axis=2)]
    convert_element_type x3 -> x0, other arithmetic: 18.3 us -> none  [the longest x1 11 us: on_device(): return (rotated, applied.astype(jnp.bfloat16))]
    dot_general x1 -> x0, matrix products: 6.87 us -> none  [on_device(): lax.dot_general(lax.all_gather(flat, 'band', axis=1, tiled=True), rotatio...]
    ppermute x2 -> x0, local copies, waits for them, and re-layouts: 4.2 us -> none  [the longest x1 2.44 us: with_halo(): lax.ppermute(tail, axis, [(i, (i + 1) % count) for i in range(ends)])]
    unnamed x25 -> x63, local copies, waits for them, and re-layouts: 6.35 us -> 2.87 us
  transfers between devices with their start and end apart: 5 -> 37, of which waited for: 2 -> 1; matrix products, arithmetic and copies ran while one was open for 6% -> 1% of each run, Pallas kernels for 0% -> 14%
where the time goes in v2:
time: 173 us; the launch traced here: 170 us
  starting transfers between devices  128 us (74%)
  Pallas kernels  33.5 us (19%)
  local copies, waits for them, and re-layouts  3.98 us (2%)
  waiting for transfers between devices  2.01 us (1%)
    ppermute x30, starting transfers between devices, on_device(): blocks[side][step * distance] = lax.ppermute(held, 'band', hops[step])  95.6 us
    pallas_call x5, Pallas kernels, rotate(): pl.pallas_call(functools.partial(rotate_kernel, first, last, begin, len(b...  28.5 us
    ppermute x1, starting transfers between devices, on_device(): keep_x = lax.ppermute(keep_x, ('dx', 'band'), near)  12.5 us
    pallas_call x1, Pallas kernels, stencil(): pl.pallas_call(stencil_kernel, in_specs=[SMEM] + [VMEM] * len(arrays), ou...  4.95 us
    ppermute x1, starting transfers between devices, on_device(): keep_y = lax.ppermute(keep_y, 'dy', [(0, 1), (1, 0)])  4.53 us
    ppermute x1, starting transfers between devices, on_device(): came = lax.ppermute(sent.reshape(points, lanes), 'band', across)  4.02 us
    ppermute x1, starting transfers between devices, on_device(): send_y = lax.ppermute(send_y, ('dy', 'band'), turn)  3.96 us
  transfers between devices with their start and end apart: 37, of which 1 were waited for; matrix products, arithmetic and copies ran while one was open for 1% of the time, Pallas kernels for 14%

profile of v2, /device:TPU:1, one launch (start us, length us, event | category | flops | bytes accessed | tf_op | source)
XLA Modules:
  0.0 170.0 jit_solution(15314297148508711507)
XLA Ops:
  0.7 1.1 constant_dynamic-slice_fusion
  1.8 4.0 %collective-permute-start.1 = (bf16[384,256]{1,0:T(8,128)(2,1)S(1)}, bf16[384,256]{1,0:T(8,128)(2,1)S(1)}, u32[]{:S(2)}, u32[]{:S(2)}) collective-permute-start(bf16[384,256]{1,0:T(8,128)(2,1)S(1)} %bitcast.13), channel_id=1, source_target_pairs={{0,16},{1,17},{2,18},{3,19},{4,20},{5,21},{6,22},{7,23},{8,24},{9,... | collective-permute-start | bytes 589832 | tf_op jit(solution)/shard_map/ppermute | solution.py:198
  5.8 3.5 %collective-permute-start.16 = (bf16[384,256]{1,0:T(8,128)(2,1)S(1)}, bf16[384,256]{1,0:T(8,128)(2,1)S(1)}, u32[]{:S(2)}, u32[]{:S(2)}) collective-permute-start(bf16[384,256]{1,0:T(8,128)(2,1)S(1)} %bitcast.10), channel_id=1, source_target_pairs={{0,1},{1,2},{2,3},{3,4},{4,5},{5,6},{6,7},{7,8},{8,9},{9,10},{10,1... | collective-permute-start | bytes 589832 | tf_op jit(solution)/shard_map/ppermute | solution.py:208
  9.4 9.5 %collective-permute-start.25 = (bf16[384,256]{1,0:T(8,128)(2,1)S(1)}, bf16[384,256]{1,0:T(8,128)(2,1)S(1)}, u32[]{:S(2)}, u32[]{:S(2)}) collective-permute-start(bf16[384,256]{1,0:T(8,128)(2,1)S(1)} %bitcast.11), channel_id=1, source_target_pairs={{0,15},{1,0},{2,1},{3,2},{4,3},{5,4},{6,5},{7,6},{8,7},{9,8},{10,9... | collective-permute-start | bytes 589832 | tf_op jit(solution)/shard_map/ppermute | solution.py:208
  18.9 0.0 collective-permute-done.1.refs_4_
  18.9 3.4 %collective-permute-start.2 = (bf16[384,256]{1,0:T(8,128)(2,1)S(1)}, bf16[384,256]{1,0:T(8,128)(2,1)S(1)}, u32[]{:S(2)}, u32[]{:S(2)}) collective-permute-start(bf16[384,256]{1,0:T(8,128)(2,1)S(1)} %collective-permute-done.1.refs_4_), channel_id=1, source_target_pairs={{0,15},{1,0},{2,1},{3,2},{4,3},{5,4},{6,5},{7,6},{8,7},{9,8},{10,9... | collective-permute-start | bytes 589832 | tf_op jit(solution)/shard_map/ppermute | solution.py:208
  22.3 1.9 %collective-permute-start.9 = (bf16[384,256]{1,0:T(8,128)(2,1)S(1)}, bf16[384,256]{1,0:T(8,128)(2,1)S(1)}, u32[]{:S(2)}, u32[]{:S(2)}) collective-permute-start(bf16[384,256]{1,0:T(8,128)(2,1)S(1)} %collective-permute-done.1.refs_4_), channel_id=1, source_target_pairs={{0,1},{1,2},{2,3},{3,4},{4,5},{5,6},{6,7},{7,8},{8,9},{9,10},{10,1... | collective-permute-start | bytes 589832 | tf_op jit(solution)/shard_map/ppermute | solution.py:208
  24.2 0.0 collective-permute-done.16.refs_6_
  24.2 1.9 %collective-permute-start.17 = (bf16[384,256]{1,0:T(8,128)(2,1)S(1)}, bf16[384,256]{1,0:T(8,128)(2,1)S(1)}, u32[]{:S(2)}, u32[]{:S(2)}) collective-permute-start(bf16[384,256]{1,0:T(8,128)(2,1)S(1)} %collective-permute-done.16.refs_6_), channel_id=1, source_target_pairs={{0,1},{1,2},{2,3},{3,4},{4,5},{5,6},{6,7},{7,8},{8,9},{9,10},{10,1... | collective-permute-start | bytes 589832 | tf_op jit(solution)/shard_map/ppermute | solution.py:208
  26.2 4.6 %collective-permute-start.26 = (bf16[384,256]{1,0:T(8,128)(2,1)S(1)}, bf16[384,256]{1,0:T(8,128)(2,1)S(1)}, u32[]{:S(2)}, u32[]{:S(2)}) collective-permute-start(bf16[384,256]{1,0:T(8,128)(2,1)S(1)} %collective-permute-done.25.refs_5_), channel_id=1, source_target_pairs={{0,15},{1,0},{2,1},{3,2},{4,3},{5,4},{6,5},{7,6},{8,7},{9,8},{10,9... | collective-permute-start | bytes 589832 | tf_op jit(solution)/shard_map/ppermute | solution.py:208
  30.7 0.0 collective-permute-done.2.refs_7_
  30.8 3.4 %collective-permute-start.3 = (bf16[384,256]{1,0:T(8,128)(2,1)S(1)}, bf16[384,256]{1,0:T(8,128)(2,1)S(1)}, u32[]{:S(2)}, u32[]{:S(2)}) collective-permute-start(bf16[384,256]{1,0:T(8,128)(2,1)S(1)} %collective-permute-done.2.refs_7_), channel_id=1, source_target_pairs={{0,15},{1,0},{2,1},{3,2},{4,3},{5,4},{6,5},{7,6},{8,7},{9,8},{10,9... | collective-permute-start | bytes 589832 | tf_op jit(solution)/shard_map/ppermute | solution.py:208
  34.1 1.9 %collective-permute-start.10 = (bf16[384,256]{1,0:T(8,128)(2,1)S(1)}, bf16[384,256]{1,0:T(8,128)(2,1)S(1)}, u32[]{:S(2)}, u32[]{:S(2)}) collective-permute-start(bf16[384,256]{1,0:T(8,128)(2,1)S(1)} %collective-permute-done.9.refs_8_), channel_id=1, source_target_pairs={{0,1},{1,2},{2,3},{3,4},{4,5},{5,6},{6,7},{7,8},{8,9},{9,10},{10,1... | collective-permute-start | bytes 589832 | tf_op jit(solution)/shard_map/ppermute | solution.py:208
  36.1 0.0 collective-permute-done.17.refs_10_
  36.1 1.9 %collective-permute-start.18 = (bf16[384,256]{1,0:T(8,128)(2,1)S(1)}, bf16[384,256]{1,0:T(8,128)(2,1)S(1)}, u32[]{:S(2)}, u32[]{:S(2)}) collective-permute-start(bf16[384,256]{1,0:T(8,128)(2,1)S(1)} %collective-permute-done.17.refs_10_), channel_id=1, source_target_pairs={{0,1},{1,2},{2,3},{3,4},{4,5},{5,6},{6,7},{7,8},{8,9},{9,10},{10,1... | collective-permute-start | bytes 589832 | tf_op jit(solution)/shard_map/ppermute | solution.py:208
  38.0 0.0 collective-permute-done.26.refs_9_
  38.0 4.6 %collective-permute-start.27 = (bf16[384,256]{1,0:T(8,128)(2,1)S(1)}, bf16[384,256]{1,0:T(8,128)(2,1)S(1)}, u32[]{:S(2)}, u32[]{:S(2)}) collective-permute-start(bf16[384,256]{1,0:T(8,128)(2,1)S(1)} %collective-permute-done.26.refs_9_), channel_id=1, source_target_pairs={{0,15},{1,0},{2,1},{3,2},{4,3},{5,4},{6,5},{7,6},{8,7},{9,8},{10,9... | collective-permute-start | bytes 589832 | tf_op jit(solution)/shard_map/ppermute | solution.py:208
  42.6 0.0 collective-permute-done.3.refs_3_
  42.6 0.0 copy-start.16
  42.6 3.4 %collective-permute-start.4 = (bf16[384,256]{1,0:T(8,128)(2,1)S(1)}, bf16[384,256]{1,0:T(8,128)(2,1)}, u32[]{:S(2)}, u32[]{:S(2)}) collective-permute-start(bf16[384,256]{1,0:T(8,128)(2,1)S(1)} %collective-permute-done.3.refs_3_), channel_id=1, source_target_pairs={{0,15},{1,0},{2,1},{3,2},{4,3},{5,4},{6,5},{7,6},{8,7},{9,8},{10,9... | collective-permute-start | bytes 589832 | tf_op jit(solution)/shard_map/ppermute | solution.py:208
  46.0 2.3 %collective-permute-start = (bf16[64,2048]{1,0:T(8,128)(2,1)S(1)}, bf16[64,2048]{1,0:T(8,128)(2,1)S(1)}, u32[]{:S(2)}, u32[]{:S(2)}) collective-permute-start(bf16[64,2048]{1,0:T(8,128)(2,1)S(1)} %copy-done), channel_id=1, source_target_pairs={{0,16},{1,17},{2,18},{3,19},{4,20},{5,21},{6,22},{7,23},{8,24},{9,... | collective-permute-start | bytes 786440 | tf_op jit(solution)/shard_map/ppermute | solution.py:199
  48.4 0.0 copy-start.18
  48.4 1.9 %collective-permute-start.11 = (bf16[384,256]{1,0:T(8,128)(2,1)S(1)}, bf16[384,256]{1,0:T(8,128)(2,1)}, u32[]{:S(2)}, u32[]{:S(2)}) collective-permute-start(bf16[384,256]{1,0:T(8,128)(2,1)S(1)} %collective-permute-done.10.refs_4_), channel_id=1, source_target_pairs={{0,1},{1,2},{2,3},{3,4},{4,5},{5,6},{6,7},{7,8},{8,9},{9,10},{10,1... | collective-permute-start | bytes 589832 | tf_op jit(solution)/shard_map/ppermute | solution.py:208
  50.4 1.9 %collective-permute-start.19 = (bf16[384,256]{1,0:T(8,128)(2,1)S(1)}, bf16[384,256]{1,0:T(8,128)(2,1)}, u32[]{:S(2)}, u32[]{:S(2)}) collective-permute-start(bf16[384,256]{1,0:T(8,128)(2,1)S(1)} %collective-permute-done.18.refs_6_), channel_id=1, source_target_pairs={{0,1},{1,2},{2,3},{3,4},{4,5},{5,6},{6,7},{7,8},{8,9},{9,10},{10,1... | collective-permute-start | bytes 589832 | tf_op jit(solution)/shard_map/ppermute | solution.py:208
  52.3 4.6 %collective-permute-start.28 = (bf16[384,256]{1,0:T(8,128)(2,1)S(1)}, bf16[384,256]{1,0:T(8,128)(2,1)}, u32[]{:S(2)}, u32[]{:S(2)}) collective-permute-start(bf16[384,256]{1,0:T(8,128)(2,1)S(1)} %collective-permute-done.27.refs_5_), channel_id=1, source_target_pairs={{0,15},{1,0},{2,1},{3,2},{4,3},{5,4},{6,5},{7,6},{8,7},{9,8},{10,9... | collective-permute-start | bytes 589832 | tf_op jit(solution)/shard_map/ppermute | solution.py:208
  56.9 3.4 %collective-permute-start.5 = (bf16[384,256]{1,0:T(8,128)(2,1)}, bf16[384,256]{1,0:T(8,128)(2,1)}, u32[]{:S(2)}, u32[]{:S(2)}) collective-permute-start(bf16[384,256]{1,0:T(8,128)(2,1)} %collective-permute-done.4.refs_7_), channel_id=1, source_target_pairs={{0,15},{1,0},{2,1},{3,2},{4,3},{5,4},{6,5},{7,6},{8,7},{9,8},{10,9... | collective-permute-start | bytes 589832 | tf_op jit(solution)/shard_map/ppermute | solution.py:208
  60.3 0.6 pad_add_fusion.refs_0_.place_ref
  61.0 2.0 %collective-permute-start.12 = (bf16[384,256]{1,0:T(8,128)(2,1)}, bf16[384,256]{1,0:T(8,128)(2,1)S(1)}, u32[]{:S(2)}, u32[]{:S(2)}) collective-permute-start(bf16[384,256]{1,0:T(8,128)(2,1)} %collective-permute-done.11.refs_8_), channel_id=1, source_target_pairs={{0,1},{1,2},{2,3},{3,4},{4,5},{5,6},{6,7},{7,8},{8,9},{9,10},{10,1... | collective-permute-start | bytes 589832 | tf_op jit(solution)/shard_map/ppermute | solution.py:208
  63.0 1.9 %collective-permute-start.20 = (bf16[384,256]{1,0:T(8,128)(2,1)}, bf16[384,256]{1,0:T(8,128)(2,1)S(1)}, u32[]{:S(2)}, u32[]{:S(2)}) collective-permute-start(bf16[384,256]{1,0:T(8,128)(2,1)} %collective-permute-done.19.refs_10_), channel_id=1, source_target_pairs={{0,1},{1,2},{2,3},{3,4},{4,5},{5,6},{6,7},{7,8},{8,9},{9,10},{10,1... | collective-permute-start | bytes 589832 | tf_op jit(solution)/shard_map/ppermute | solution.py:208
  65.0 4.6 %collective-permute-start.29 = (bf16[384,256]{1,0:T(8,128)(2,1)}, bf16[384,256]{1,0:T(8,128)(2,1)}, u32[]{:S(2)}, u32[]{:S(2)}) collective-permute-start(bf16[384,256]{1,0:T(8,128)(2,1)} %collective-permute-done.28.refs_9_), channel_id=1, source_target_pairs={{0,15},{1,0},{2,1},{3,2},{4,3},{5,4},{6,5},{7,6},{8,7},{9,8},{10,9... | collective-permute-start | bytes 589832 | tf_op jit(solution)/shard_map/ppermute | solution.py:208
  69.6 3.4 %collective-permute-start.6 = (bf16[384,256]{1,0:T(8,128)(2,1)}, bf16[384,256]{1,0:T(8,128)(2,1)S(1)}, u32[]{:S(2)}, u32[]{:S(2)}) collective-permute-start(bf16[384,256]{1,0:T(8,128)(2,1)} %collective-permute-done.5.refs_3_), channel_id=1, source_target_pairs={{0,15},{1,0},{2,1},{3,2},{4,3},{5,4},{6,5},{7,6},{8,7},{9,8},{10,9... | collective-permute-start | bytes 589832 | tf_op jit(solution)/shard_map/ppermute | solution.py:208
  72.9 0.5 fusion.refs_1_
  73.4 1.9 %collective-permute-start.13 = (bf16[384,256]{1,0:T(8,128)(2,1)S(1)}, bf16[384,256]{1,0:T(8,128)(2,1)S(1)}, u32[]{:S(2)}, u32[]{:S(2)}) collective-permute-start(bf16[384,256]{1,0:T(8,128)(2,1)S(1)} %collective-permute-done.12.refs_4_), channel_id=1, source_target_pairs={{0,1},{1,2},{2,3},{3,4},{4,5},{5,6},{6,7},{7,8},{8,9},{9,10},{10,1... | collective-permute-start | bytes 589832 | tf_op jit(solution)/shard_map/ppermute | solution.py:208
  75.4 1.9 %collective-permute-start.21 = (bf16[384,256]{1,0:T(8,128)(2,1)S(1)}, bf16[384,256]{1,0:T(8,128)(2,1)}, u32[]{:S(2)}, u32[]{:S(2)}) collective-permute-start(bf16[384,256]{1,0:T(8,128)(2,1)S(1)} %collective-permute-done.20.refs_6_), channel_id=1, source_target_pairs={{0,1},{1,2},{2,3},{3,4},{4,5},{5,6},{6,7},{7,8},{8,9},{9,10},{10,1... | collective-permute-start | bytes 589832 | tf_op jit(solution)/shard_map/ppermute | solution.py:208
  77.3 4.6 %collective-permute-start.30 = (bf16[384,256]{1,0:T(8,128)(2,1)}, bf16[384,256]{1,0:T(8,128)(2,1)}, u32[]{:S(2)}, u32[]{:S(2)}) collective-permute-start(bf16[384,256]{1,0:T(8,128)(2,1)} %collective-permute-done.29.refs_5_), channel_id=1, source_target_pairs={{0,15},{1,0},{2,1},{3,2},{4,3},{5,4},{6,5},{7,6},{8,7},{9,8},{10,9... | collective-permute-start | bytes 589832 | tf_op jit(solution)/shard_map/ppermute | solution.py:208
  81.9 3.4 %collective-permute-start.7 = (bf16[384,256]{1,0:T(8,128)(2,1)S(1)}, bf16[384,256]{1,0:T(8,128)(2,1)}, u32[]{:S(2)}, u32[]{:S(2)}) collective-permute-start(bf16[384,256]{1,0:T(8,128)(2,1)S(1)} %collective-permute-done.6.refs_7_), channel_id=1, source_target_pairs={{0,15},{1,0},{2,1},{3,2},{4,3},{5,4},{6,5},{7,6},{8,7},{9,8},{10,9... | collective-permute-start | bytes 589832 | tf_op jit(solution)/shard_map/ppermute | solution.py:208
  85.4 1.9 %collective-permute-start.14 = (bf16[384,256]{1,0:T(8,128)(2,1)S(1)}, bf16[384,256]{1,0:T(8,128)(2,1)S(1)}, u32[]{:S(2)}, u32[]{:S(2)}) collective-permute-start(bf16[384,256]{1,0:T(8,128)(2,1)S(1)} %collective-permute-done.13.refs_8_), channel_id=1, source_target_pairs={{0,1},{1,2},{2,3},{3,4},{4,5},{5,6},{6,7},{7,8},{8,9},{9,10},{10,1... | collective-permute-start | bytes 589832 | tf_op jit(solution)/shard_map/ppermute | solution.py:208
  87.3 1.9 %collective-permute-start.22 = (bf16[384,256]{1,0:T(8,128)(2,1)}, bf16[384,256]{1,0:T(8,128)(2,1)}, u32[]{:S(2)}, u32[]{:S(2)}) collective-permute-start(bf16[384,256]{1,0:T(8,128)(2,1)} %collective-permute-done.21.refs_10_), channel_id=1, source_target_pairs={{0,1},{1,2},{2,3},{3,4},{4,5},{5,6},{6,7},{7,8},{8,9},{9,10},{10,1... | collective-permute-start | bytes 589832 | tf_op jit(solution)/shard_map/ppermute | solution.py:208
  89.3 4.6 %collective-permute-start.8 = (bf16[384,256]{1,0:T(8,128)(2,1)}, bf16[384,256]{1,0:T(8,128)(2,1)S(1)}, u32[]{:S(2)}, u32[]{:S(2)}) collective-permute-start(bf16[384,256]{1,0:T(8,128)(2,1)} %collective-permute-done.7.refs_3_), channel_id=1, source_target_pairs={{0,15},{1,0},{2,1},{3,2},{4,3},{5,4},{6,5},{7,6},{8,7},{9,8},{10,9... | collective-permute-start | bytes 589832 | tf_op jit(solution)/shard_map/ppermute | solution.py:208
  93.9 6.7 %rotate.5 = (f32[384,512]{1,0:T(8,128)}, f32[16,48,256]{2,1,0:T(8,128)}) custom-call(s32[2]{0:T(128)} %pad_add_fusion.refs_0_.place_ref, s32[32]{0:T(128)} %fusion.refs_1_, bf16[128,2048]{1,0:T(8,128)(2,1)} %copy-done.3, bf16[384,256]{1,0:T(8,128)(2,1)} %bitcast.12, bf16[384,256]{1,0:T(8,128)(2,1)} %copy-done.10, bf16[384,256]{1,0:T(8,128)(2,1)} %copy-done.12, ...), custom_call_target="tpu_custom_call" | custom-call | flops 1600000000 | bytes 3145728 | tf_op jit(solution)/shard_map/rotate/pallas_call | solution.py:112
  100.7 3.4 %collective-permute-start.31 = (bf16[384,256]{1,0:T(8,128)(2,1)}, bf16[384,256]{1,0:T(8,128)(2,1)S(1)}, u32[]{:S(2)}, u32[]{:S(2)}) collective-permute-start(bf16[384,256]{1,0:T(8,128)(2,1)} %collective-permute-done.30.refs_9_), channel_id=1, source_target_pairs={{0,15},{1,0},{2,1},{3,2},{4,3},{5,4},{6,5},{7,6},{8,7},{9,8},{10,9... | collective-permute-start | bytes 589832 | tf_op jit(solution)/shard_map/ppermute | solution.py:208
  104.0 6.5 %rotate.6.refs_11_ = f32[384,512]{1,0:T(8,128)} custom-call(s32[2]{0:T(128)} %pad_add_fusion.refs_0_.place_ref, s32[32]{0:T(128)} %fusion.refs_1_, bf16[128,2048]{1,0:T(8,128)(2,1)} %copy-done.3, bf16[384,256]{1,0:T(8,128)(2,1)} %copy-done.16, bf16[384,256]{1,0:T(8,128)(2,1)} %copy-done.18, ...), custom_call_target="tpu_custom_call", output_to_operand_aliasing={{}: (11, {})} | custom-call | flops 1600000000 | bytes 3145728 | tf_op jit(solution)/shard_map/rotate/pallas_call | solution.py:112
  110.5 1.9 %collective-permute-start.15 = (bf16[384,256]{1,0:T(8,128)(2,1)S(1)}, bf16[384,256]{1,0:T(8,128)(2,1)S(1)}, u32[]{:S(2)}, u32[]{:S(2)}) collective-permute-start(bf16[384,256]{1,0:T(8,128)(2,1)S(1)} %collective-permute-done.14.refs_4_), channel_id=1, source_target_pairs={{0,1},{1,2},{2,3},{3,4},{4,5},{5,6},{6,7},{7,8},{8,9},{9,10},{10,1... | collective-permute-start | bytes 589832 | tf_op jit(solution)/shard_map/ppermute | solution.py:208
  112.5 1.9 %collective-permute-start.23 = (bf16[384,256]{1,0:T(8,128)(2,1)}, bf16[384,256]{1,0:T(8,128)(2,1)S(1)}, u32[]{:S(2)}, u32[]{:S(2)}) collective-permute-start(bf16[384,256]{1,0:T(8,128)(2,1)} %collective-permute-done.22.refs_6_), channel_id=1, source_target_pairs={{0,1},{1,2},{2,3},{3,4},{4,5},{5,6},{6,7},{7,8},{8,9},{9,10},{10,1... | collective-permute-start | bytes 589832 | tf_op jit(solution)/shard_map/ppermute | solution.py:208
  114.4 0.0 copy-start.25
  114.4 4.6 %collective-permute-start.24 = (bf16[384,256]{1,0:T(8,128)(2,1)S(1)}, bf16[384,256]{1,0:T(8,128)(2,1)S(1)}, u32[]{:S(2)}, u32[]{:S(2)}) collective-permute-start(bf16[384,256]{1,0:T(8,128)(2,1)S(1)} %collective-permute-done.8.refs_3_), channel_id=1, source_target_pairs={{0,15},{1,0},{2,1},{3,2},{4,3},{5,4},{6,5},{7,6},{8,7},{9,8},{10,9... | collective-permute-start | bytes 589832 | tf_op jit(solution)/shard_map/ppermute | solution.py:208
  119.0 6.5 %rotate.7.refs_7_ = f32[384,512]{1,0:T(8,128)} custom-call(s32[2]{0:T(128)} %pad_add_fusion.refs_0_.place_ref, s32[32]{0:T(128)} %fusion.refs_1_, bf16[128,2048]{1,0:T(8,128)(2,1)} %copy-done.3, bf16[384,256]{1,0:T(8,128)(2,1)} %collective-permute-done.5.refs_3_, bf16[384,256]{1,0:T(8,128)(2,1)} %copy-done.21, ...), custom_call_target="tpu_custom_call", output_to_operand_aliasing={{}: (11, {})} | custom-call | flops 1600000000 | bytes 3145728 | tf_op jit(solution)/shard_map/rotate/pallas_call | solution.py:112
  125.5 0.7 copy-done.28
  126.2 4.4 %rotate.8.refs_7_ = f32[384,512]{1,0:T(8,128)} custom-call(s32[2]{0:T(128)} %pad_add_fusion.refs_0_.place_ref, s32[32]{0:T(128)} %fusion.refs_1_, bf16[128,2048]{1,0:T(8,128)(2,1)} %copy-done.3, bf16[384,256]{1,0:T(8,128)(2,1)} %collective-permute-done.7.refs_3_, bf16[384,256]{1,0:T(8,128)(2,1)} %copy-done.26, ...), custom_call_target="tpu_custom_call", output_to_operand_aliasing={{}: (7, {})} | custom-call | flops 800000000 | bytes 3145728 | tf_op jit(solution)/shard_map/rotate/pallas_call | solution.py:112
  130.7 0.6 copy-done.27
  131.3 0.1 copy-done.29
  131.4 0.7 copy-done.30
  132.0 4.4 %rotate.9 = (bf16[384,256]{1,0:T(8,128)(2,1)}, bf16[384,256]{1,0:T(8,128)(2,1)}, bf16[192,256]{1,0:T(8,128)(2,1)}, bf16[192,256]{1,0:T(8,128)(2,1)}, bf16[8,4,25...) custom-call(s32[2]{0:T(128)} %pad_add_fusion.refs_0_.place_ref, s32[32]{0:T(128)} %fusion.refs_1_, ...), custom_call_target="tpu_custom_call" | custom-call | flops 800000000 | bytes 3145728 | tf_op jit(solution)/shard_map/rotate/pallas_call | solution.py:112
  136.5 2.9 %collective-permute-start.32 = (bf16[384,256]{1,0:T(8,128)(2,1)}, bf16[384,256]{1,0:T(8,128)(2,1)S(1)}, u32[]{:S(2)}, u32[]{:S(2)}) collective-permute-start(bf16[384,256]{1,0:T(8,128)(2,1)} %get-tuple-element.12), channel_id=1, source_target_pairs={{0,16},{1,17},{2,18},{3,19},{4,20},{5,21},{6,22},{7,23},{8,24},{9,... | collective-permute-start | bytes 589832 | tf_op jit(solution)/shard_map/ppermute | solution.py:240
  139.4 12.5 %collective-permute-start.33 = (bf16[192,256]{1,0:T(8,128)(2,1)}, bf16[192,256]{1,0:T(8,128)(2,1)S(1)}, u32[]{:S(2)}, u32[]{:S(2)}) collective-permute-start(bf16[192,256]{1,0:T(8,128)(2,1)} %get-tuple-element.13), channel_id=1, source_target_pairs={{16,80},{64,0},{17,81},{65,1},{18,82},{66,2},{19,83},{67,3},{20,84... | collective-permute-start | bytes 294920 | tf_op jit(solution)/shard_map/ppermute | solution.py:241
  151.9 1.9 %collective-permute-start.34 = (bf16[192,256]{1,0:T(8,128)(2,1)}, bf16[192,256]{1,0:T(8,128)(2,1)S(1)}, u32[]{:S(2)}, u32[]{:S(2)}) collective-permute-start(bf16[192,256]{1,0:T(8,128)(2,1)} %get-tuple-element.14), channel_id=1, source_target_pairs={{16,64},{64,16},{17,65},{65,17},{18,66},{66,18},{19,67},{67,19},{2... | collective-permute-start | bytes 294920 | tf_op jit(solution)/shard_map/ppermute | solution.py:242
  153.8 4.5 %collective-permute-start.35 = (bf16[8,4,256]{2,1,0:T(4,128)(2,1)}, bf16[8,4,256]{2,1,0:T(4,128)(2,1)S(1)}, u32[]{:S(2)}, u32[]{:S(2)}) collective-permute-start(bf16[8,4,256]{2,1,0:T(4,128)(2,1)} %get-tuple-element.15), channel_id=1, source_target_pairs={{0,32},{32,0},{1,33},{33,1},{2,34},{34,2},{3,35},{35,3},{4,36},{36... | collective-permute-start | bytes 49160 | tf_op jit(solution)/shard_map/ppermute | solution.py:243
  158.4 4.0 %collective-permute-start.36 = (bf16[8,4,256]{2,1,0:T(4,128)(2,1)}, bf16[8,4,256]{2,1,0:T(4,128)(2,1)S(1)}, u32[]{:S(2)}, u32[]{:S(2)}) collective-permute-start(bf16[8,4,256]{2,1,0:T(4,128)(2,1)} %get-tuple-element.16), channel_id=1, source_target_pairs={{0,48},{1,49},{2,50},{3,51},{4,52},{5,53},{6,54},{7,55},{8,56},{9,... | collective-permute-start | bytes 49160 | tf_op jit(solution)/shard_map/ppermute | solution.py:249
  162.4 1.9 %collective-permute-done.36.send_y_ref = bf16[8,4,256]{2,1,0:T(4,128)(2,1)S(1)} collective-permute-done((bf16[8,4,256]{2,1,0:T(4,128)(2,1)}, bf16[8,4,256]{2,1,0:T(4,128)(2,1)S(1)}, u32[]{:S(2)}, u32[]{:S(2)}) %collective-permute-start.36) | collective-permute-done | bytes 16416 | tf_op jit(solution)/shard_map/ppermute | solution.py:249
  164.3 0.5 copy-done.7
  164.9 0.0 copy-done.4
  164.9 0.1 copy-done.5
  165.0 0.0 copy-done.1
  165.0 4.9 %stencil.1 = (bf16[16,48,256]{2,1,0:T(8,128)(2,1)}, bf16[16,48,256]{2,1,0:T(8,128)(2,1)}) custom-call(s32[2]{0:T(128)} %pad_add_fusion.refs_0_.place_ref, bf16[8,48,256]{2,1,0:T(8,128)(2,1)} %bitcast.8, bf16[8,48,256]{2,1,0:T(8,128)(2,1)} %bitcast.9, bf16[4,48,256]{2,1,0:T(8,128)(2,1)} %bitcast.14, bf16[4,48,256]{2,1,0:T(8,128)(2,1)} %bitcast.15, ...), custom_call_target="tpu_custom_call" | custom-call | tf_op jit(solution)/shard_map/stencil/pallas_call | solution.py:171
  (83 shorter events, 0.2 us)
Async XLA Ops:
  0.7 45.4 %copy-start = (bf16[64,2048]{1,0:T(8,128)(2,1)S(1)}, bf16[64,2048]{1,0:T(8,128)(2,1)}, u32[]{:S(2)}) copy-start(bf16[64,2048]{1,0:T(8,128)(2,1)} %param.6) | copy-start | bytes 786436
  1.8 58.5 %copy-start.2 = (bf16[8,48,256]{2,1,0:T(8,128)(2,1)}, bf16[8,48,256]{2,1,0:T(8,128)(2,1)S(1)}, u32[]{:S(2)}) copy-start(bf16[8,48,256]{2,1,0:T(8,128)(2,1)S(1)} %get-tuple-element.18) | copy-start | bytes 589828
  1.8 17.1 %collective-permute-start.1 = (bf16[384,256]{1,0:T(8,128)(2,1)S(1)}, bf16[384,256]{1,0:T(8,128)(2,1)S(1)}, u32[]{:S(2)}, u32[]{:S(2)}) collective-permute-start(bf16[384,256]{1,0:T(8,128)(2,1)S(1)} %bitcast.13), channel_id=1, source_target_pairs={{0,16},{1,17},{2,18},{3,19},{4,20},{5,21},{6,22},{7,23},{8,24},{9,... | collective-permute-start | bytes 589832 | tf_op jit(solution)/shard_map/ppermute | solution.py:198
  5.8 18.4 %collective-permute-start.16 = (bf16[384,256]{1,0:T(8,128)(2,1)S(1)}, bf16[384,256]{1,0:T(8,128)(2,1)S(1)}, u32[]{:S(2)}, u32[]{:S(2)}) collective-permute-start(bf16[384,256]{1,0:T(8,128)(2,1)S(1)} %bitcast.10), channel_id=1, source_target_pairs={{0,1},{1,2},{2,3},{3,4},{4,5},{5,6},{6,7},{7,8},{8,9},{9,10},{10,1... | collective-permute-start | bytes 589832 | tf_op jit(solution)/shard_map/ppermute | solution.py:208
  9.4 16.8 %collective-permute-start.25 = (bf16[384,256]{1,0:T(8,128)(2,1)S(1)}, bf16[384,256]{1,0:T(8,128)(2,1)S(1)}, u32[]{:S(2)}, u32[]{:S(2)}) collective-permute-start(bf16[384,256]{1,0:T(8,128)(2,1)S(1)} %bitcast.11), channel_id=1, source_target_pairs={{0,15},{1,0},{2,1},{3,2},{4,3},{5,4},{6,5},{7,6},{8,7},{9,8},{10,9... | collective-permute-start | bytes 589832 | tf_op jit(solution)/shard_map/ppermute | solution.py:208
  18.9 41.4 %copy-start.10 = (bf16[384,256]{1,0:T(8,128)(2,1)}, bf16[384,256]{1,0:T(8,128)(2,1)S(1)}, u32[]{:S(2)}) copy-start(bf16[384,256]{1,0:T(8,128)(2,1)S(1)} %collective-permute-done.1.refs_4_) | copy-start | bytes 589828
  18.9 11.9 %collective-permute-start.2 = (bf16[384,256]{1,0:T(8,128)(2,1)S(1)}, bf16[384,256]{1,0:T(8,128)(2,1)S(1)}, u32[]{:S(2)}, u32[]{:S(2)}) collective-permute-start(bf16[384,256]{1,0:T(8,128)(2,1)S(1)} %collective-permute-done.1.refs_4_), channel_id=1, source_target_pairs={{0,15},{1,0},{2,1},{3,2},{4,3},{5,4},{6,5},{7,6},{8,7},{9,8},{10,9... | collective-permute-start | bytes 589832 | tf_op jit(solution)/shard_map/ppermute | solution.py:208
  22.3 11.9 %collective-permute-start.9 = (bf16[384,256]{1,0:T(8,128)(2,1)S(1)}, bf16[384,256]{1,0:T(8,128)(2,1)S(1)}, u32[]{:S(2)}, u32[]{:S(2)}) collective-permute-start(bf16[384,256]{1,0:T(8,128)(2,1)S(1)} %collective-permute-done.1.refs_4_), channel_id=1, source_target_pairs={{0,1},{1,2},{2,3},{3,4},{4,5},{5,6},{6,7},{7,8},{8,9},{9,10},{10,1... | collective-permute-start | bytes 589832 | tf_op jit(solution)/shard_map/ppermute | solution.py:208
  24.2 69.7 %copy-start.11 = (bf16[384,256]{1,0:T(8,128)(2,1)}, bf16[384,256]{1,0:T(8,128)(2,1)S(1)}, u32[]{:S(2)}) copy-start(bf16[384,256]{1,0:T(8,128)(2,1)S(1)} %collective-permute-done.16.refs_6_) | copy-start | bytes 589828
  24.2 11.9 %collective-permute-start.17 = (bf16[384,256]{1,0:T(8,128)(2,1)S(1)}, bf16[384,256]{1,0:T(8,128)(2,1)S(1)}, u32[]{:S(2)}, u32[]{:S(2)}) collective-permute-start(bf16[384,256]{1,0:T(8,128)(2,1)S(1)} %collective-permute-done.16.refs_6_), channel_id=1, source_target_pairs={{0,1},{1,2},{2,3},{3,4},{4,5},{5,6},{6,7},{7,8},{8,9},{9,10},{10,1... | collective-permute-start | bytes 589832 | tf_op jit(solution)/shard_map/ppermute | solution.py:208
  26.1 67.7 %copy-start.12 = (bf16[384,256]{1,0:T(8,128)(2,1)}, bf16[384,256]{1,0:T(8,128)(2,1)S(1)}, u32[]{:S(2)}) copy-start(bf16[384,256]{1,0:T(8,128)(2,1)S(1)} %collective-permute-done.25.refs_5_) | copy-start | bytes 589828
  26.2 11.9 %collective-permute-start.26 = (bf16[384,256]{1,0:T(8,128)(2,1)S(1)}, bf16[384,256]{1,0:T(8,128)(2,1)S(1)}, u32[]{:S(2)}, u32[]{:S(2)}) collective-permute-start(bf16[384,256]{1,0:T(8,128)(2,1)S(1)} %collective-permute-done.25.refs_5_), channel_id=1, source_target_pairs={{0,15},{1,0},{2,1},{3,2},{4,3},{5,4},{6,5},{7,6},{8,7},{9,8},{10,9... | collective-permute-start | bytes 589832 | tf_op jit(solution)/shard_map/ppermute | solution.py:208
  30.7 63.1 %copy-start.13 = (bf16[384,256]{1,0:T(8,128)(2,1)}, bf16[384,256]{1,0:T(8,128)(2,1)S(1)}, u32[]{:S(2)}) copy-start(bf16[384,256]{1,0:T(8,128)(2,1)S(1)} %collective-permute-done.2.refs_7_) | copy-start | bytes 589828
  30.8 11.9 %collective-permute-start.3 = (bf16[384,256]{1,0:T(8,128)(2,1)S(1)}, bf16[384,256]{1,0:T(8,128)(2,1)S(1)}, u32[]{:S(2)}, u32[]{:S(2)}) collective-permute-start(bf16[384,256]{1,0:T(8,128)(2,1)S(1)} %collective-permute-done.2.refs_7_), channel_id=1, source_target_pairs={{0,15},{1,0},{2,1},{3,2},{4,3},{5,4},{6,5},{7,6},{8,7},{9,8},{10,9... | collective-permute-start | bytes 589832 | tf_op jit(solution)/shard_map/ppermute | solution.py:208
  34.1 59.7 %copy-start.14 = (bf16[384,256]{1,0:T(8,128)(2,1)}, bf16[384,256]{1,0:T(8,128)(2,1)S(1)}, u32[]{:S(2)}) copy-start(bf16[384,256]{1,0:T(8,128)(2,1)S(1)} %collective-permute-done.9.refs_8_) | copy-start | bytes 589828
  34.1 14.2 %collective-permute-start.10 = (bf16[384,256]{1,0:T(8,128)(2,1)S(1)}, bf16[384,256]{1,0:T(8,128)(2,1)S(1)}, u32[]{:S(2)}, u32[]{:S(2)}) collective-permute-start(bf16[384,256]{1,0:T(8,128)(2,1)S(1)} %collective-permute-done.9.refs_8_), channel_id=1, source_target_pairs={{0,1},{1,2},{2,3},{3,4},{4,5},{5,6},{6,7},{7,8},{8,9},{9,10},{10,1... | collective-permute-start | bytes 589832 | tf_op jit(solution)/shard_map/ppermute | solution.py:208
  36.1 57.8 %copy-start.15 = (bf16[384,256]{1,0:T(8,128)(2,1)}, bf16[384,256]{1,0:T(8,128)(2,1)S(1)}, u32[]{:S(2)}) copy-start(bf16[384,256]{1,0:T(8,128)(2,1)S(1)} %collective-permute-done.17.refs_10_) | copy-start | bytes 589828
  36.1 14.2 %collective-permute-start.18 = (bf16[384,256]{1,0:T(8,128)(2,1)S(1)}, bf16[384,256]{1,0:T(8,128)(2,1)S(1)}, u32[]{:S(2)}, u32[]{:S(2)}) collective-permute-start(bf16[384,256]{1,0:T(8,128)(2,1)S(1)} %collective-permute-done.17.refs_10_), channel_id=1, source_target_pairs={{0,1},{1,2},{2,3},{3,4},{4,5},{5,6},{6,7},{7,8},{8,9},{9,10},{10,1... | collective-permute-start | bytes 589832 | tf_op jit(solution)/shard_map/ppermute | solution.py:208
  38.0 55.9 %copy-start.17 = (bf16[384,256]{1,0:T(8,128)(2,1)}, bf16[384,256]{1,0:T(8,128)(2,1)S(1)}, u32[]{:S(2)}) copy-start(bf16[384,256]{1,0:T(8,128)(2,1)S(1)} %collective-permute-done.26.refs_9_) | copy-start | bytes 589828
  38.0 14.2 %collective-permute-start.27 = (bf16[384,256]{1,0:T(8,128)(2,1)S(1)}, bf16[384,256]{1,0:T(8,128)(2,1)S(1)}, u32[]{:S(2)}, u32[]{:S(2)}) collective-permute-start(bf16[384,256]{1,0:T(8,128)(2,1)S(1)} %collective-permute-done.26.refs_9_), channel_id=1, source_target_pairs={{0,15},{1,0},{2,1},{3,2},{4,3},{5,4},{6,5},{7,6},{8,7},{9,8},{10,9... | collective-permute-start | bytes 589832 | tf_op jit(solution)/shard_map/ppermute | solution.py:208
  42.6 58.0 %copy-start.16 = (bf16[384,256]{1,0:T(8,128)(2,1)}, bf16[384,256]{1,0:T(8,128)(2,1)S(1)}, u32[]{:S(2)}) copy-start(bf16[384,256]{1,0:T(8,128)(2,1)S(1)} %collective-permute-done.3.refs_3_) | copy-start | bytes 589828
  42.6 14.2 %collective-permute-start.4 = (bf16[384,256]{1,0:T(8,128)(2,1)S(1)}, bf16[384,256]{1,0:T(8,128)(2,1)}, u32[]{:S(2)}, u32[]{:S(2)}) collective-permute-start(bf16[384,256]{1,0:T(8,128)(2,1)S(1)} %collective-permute-done.3.refs_3_), channel_id=1, source_target_pairs={{0,15},{1,0},{2,1},{3,2},{4,3},{5,4},{6,5},{7,6},{8,7},{9,8},{10,9... | collective-permute-start | bytes 589832 | tf_op jit(solution)/shard_map/ppermute | solution.py:208
  46.0 39.3 %collective-permute-start = (bf16[64,2048]{1,0:T(8,128)(2,1)S(1)}, bf16[64,2048]{1,0:T(8,128)(2,1)S(1)}, u32[]{:S(2)}, u32[]{:S(2)}) collective-permute-start(bf16[64,2048]{1,0:T(8,128)(2,1)S(1)} %copy-done), channel_id=1, source_target_pairs={{0,16},{1,17},{2,18},{3,19},{4,20},{5,21},{6,22},{7,23},{8,24},{9,... | collective-permute-start | bytes 786440 | tf_op jit(solution)/shard_map/ppermute | solution.py:199
  48.4 52.2 %copy-start.18 = (bf16[384,256]{1,0:T(8,128)(2,1)}, bf16[384,256]{1,0:T(8,128)(2,1)S(1)}, u32[]{:S(2)}) copy-start(bf16[384,256]{1,0:T(8,128)(2,1)S(1)} %collective-permute-done.10.refs_4_) | copy-start | bytes 589828
  48.4 12.6 %collective-permute-start.11 = (bf16[384,256]{1,0:T(8,128)(2,1)S(1)}, bf16[384,256]{1,0:T(8,128)(2,1)}, u32[]{:S(2)}, u32[]{:S(2)}) collective-permute-start(bf16[384,256]{1,0:T(8,128)(2,1)S(1)} %collective-permute-done.10.refs_4_), channel_id=1, source_target_pairs={{0,1},{1,2},{2,3},{3,4},{4,5},{5,6},{6,7},{7,8},{8,9},{9,10},{10,1... | collective-permute-start | bytes 589832 | tf_op jit(solution)/shard_map/ppermute | solution.py:208
  50.3 50.3 %copy-start.19 = (bf16[384,256]{1,0:T(8,128)(2,1)}, bf16[384,256]{1,0:T(8,128)(2,1)S(1)}, u32[]{:S(2)}) copy-start(bf16[384,256]{1,0:T(8,128)(2,1)S(1)} %collective-permute-done.18.refs_6_) | copy-start | bytes 589828
  50.4 12.7 %collective-permute-start.19 = (bf16[384,256]{1,0:T(8,128)(2,1)S(1)}, bf16[384,256]{1,0:T(8,128)(2,1)}, u32[]{:S(2)}, u32[]{:S(2)}) collective-permute-start(bf16[384,256]{1,0:T(8,128)(2,1)S(1)} %collective-permute-done.18.refs_6_), channel_id=1, source_target_pairs={{0,1},{1,2},{2,3},{3,4},{4,5},{5,6},{6,7},{7,8},{8,9},{9,10},{10,1... | collective-permute-start | bytes 589832 | tf_op jit(solution)/shard_map/ppermute | solution.py:208
  52.3 48.3 %copy-start.20 = (bf16[384,256]{1,0:T(8,128)(2,1)}, bf16[384,256]{1,0:T(8,128)(2,1)S(1)}, u32[]{:S(2)}) copy-start(bf16[384,256]{1,0:T(8,128)(2,1)S(1)} %collective-permute-done.27.refs_5_) | copy-start | bytes 589828
  52.3 12.7 %collective-permute-start.28 = (bf16[384,256]{1,0:T(8,128)(2,1)S(1)}, bf16[384,256]{1,0:T(8,128)(2,1)}, u32[]{:S(2)}, u32[]{:S(2)}) collective-permute-start(bf16[384,256]{1,0:T(8,128)(2,1)S(1)} %collective-permute-done.27.refs_5_), channel_id=1, source_target_pairs={{0,15},{1,0},{2,1},{3,2},{4,3},{5,4},{6,5},{7,6},{8,7},{9,8},{10,9... | collective-permute-start | bytes 589832 | tf_op jit(solution)/shard_map/ppermute | solution.py:208
  56.9 12.7 %collective-permute-start.5 = (bf16[384,256]{1,0:T(8,128)(2,1)}, bf16[384,256]{1,0:T(8,128)(2,1)}, u32[]{:S(2)}, u32[]{:S(2)}) collective-permute-start(bf16[384,256]{1,0:T(8,128)(2,1)} %collective-permute-done.4.refs_7_), channel_id=1, source_target_pairs={{0,15},{1,0},{2,1},{3,2},{4,3},{5,4},{6,5},{7,6},{8,7},{9,8},{10,9... | collective-permute-start | bytes 589832 | tf_op jit(solution)/shard_map/ppermute | solution.py:208
  61.0 12.0 %copy-start.8 = (s32[32]{0:T(128)S(1)}, s32[32]{0:T(128)}, u32[]{:S(2)}) copy-start(s32[32]{0:T(128)} %constant.62.clone) | copy-start | bytes 388
  61.0 12.0 %copy-start.9 = (s32[32]{0:T(128)S(1)}, s32[32]{0:T(128)}, u32[]{:S(2)}) copy-start(s32[32]{0:T(128)} %constant.64) | copy-start | bytes 388
  61.0 12.5 %collective-permute-start.12 = (bf16[384,256]{1,0:T(8,128)(2,1)}, bf16[384,256]{1,0:T(8,128)(2,1)S(1)}, u32[]{:S(2)}, u32[]{:S(2)}) collective-permute-start(bf16[384,256]{1,0:T(8,128)(2,1)} %collective-permute-done.11.refs_8_), channel_id=1, source_target_pairs={{0,1},{1,2},{2,3},{3,4},{4,5},{5,6},{6,7},{7,8},{8,9},{9,10},{10,1... | collective-permute-start | bytes 589832 | tf_op jit(solution)/shard_map/ppermute | solution.py:208
  63.0 12.3 %collective-permute-start.20 = (bf16[384,256]{1,0:T(8,128)(2,1)}, bf16[384,256]{1,0:T(8,128)(2,1)S(1)}, u32[]{:S(2)}, u32[]{:S(2)}) collective-permute-start(bf16[384,256]{1,0:T(8,128)(2,1)} %collective-permute-done.19.refs_10_), channel_id=1, source_target_pairs={{0,1},{1,2},{2,3},{3,4},{4,5},{5,6},{6,7},{7,8},{8,9},{9,10},{10,1... | collective-permute-start | bytes 589832 | tf_op jit(solution)/shard_map/ppermute | solution.py:208
  65.0 12.4 %collective-permute-start.29 = (bf16[384,256]{1,0:T(8,128)(2,1)}, bf16[384,256]{1,0:T(8,128)(2,1)}, u32[]{:S(2)}, u32[]{:S(2)}) collective-permute-start(bf16[384,256]{1,0:T(8,128)(2,1)} %collective-permute-done.28.refs_9_), channel_id=1, source_target_pairs={{0,15},{1,0},{2,1},{3,2},{4,3},{5,4},{6,5},{7,6},{8,7},{9,8},{10,9... | collective-permute-start | bytes 589832 | tf_op jit(solution)/shard_map/ppermute | solution.py:208
  69.6 12.4 %collective-permute-start.6 = (bf16[384,256]{1,0:T(8,128)(2,1)}, bf16[384,256]{1,0:T(8,128)(2,1)S(1)}, u32[]{:S(2)}, u32[]{:S(2)}) collective-permute-start(bf16[384,256]{1,0:T(8,128)(2,1)} %collective-permute-done.5.refs_3_), channel_id=1, source_target_pairs={{0,15},{1,0},{2,1},{3,2},{4,3},{5,4},{6,5},{7,6},{8,7},{9,8},{10,9... | collective-permute-start | bytes 589832 | tf_op jit(solution)/shard_map/ppermute | solution.py:208
  73.4 27.2 %copy-start.21 = (bf16[384,256]{1,0:T(8,128)(2,1)}, bf16[384,256]{1,0:T(8,128)(2,1)S(1)}, u32[]{:S(2)}) copy-start(bf16[384,256]{1,0:T(8,128)(2,1)S(1)} %collective-permute-done.12.refs_4_) | copy-start | bytes 589828
  73.4 11.9 %collective-permute-start.13 = (bf16[384,256]{1,0:T(8,128)(2,1)S(1)}, bf16[384,256]{1,0:T(8,128)(2,1)S(1)}, u32[]{:S(2)}, u32[]{:S(2)}) collective-permute-start(bf16[384,256]{1,0:T(8,128)(2,1)S(1)} %collective-permute-done.12.refs_4_), channel_id=1, source_target_pairs={{0,1},{1,2},{2,3},{3,4},{4,5},{5,6},{6,7},{7,8},{8,9},{9,10},{10,1... | collective-permute-start | bytes 589832 | tf_op jit(solution)/shard_map/ppermute | solution.py:208
  75.4 10.0 %copy-start.22 = (bf16[384,256]{1,0:T(8,128)(2,1)}, bf16[384,256]{1,0:T(8,128)(2,1)S(1)}, u32[]{:S(2)}) copy-start(bf16[384,256]{1,0:T(8,128)(2,1)S(1)} %collective-permute-done.20.refs_6_) | copy-start | bytes 589828
  75.4 11.9 %collective-permute-start.21 = (bf16[384,256]{1,0:T(8,128)(2,1)S(1)}, bf16[384,256]{1,0:T(8,128)(2,1)}, u32[]{:S(2)}, u32[]{:S(2)}) collective-permute-start(bf16[384,256]{1,0:T(8,128)(2,1)S(1)} %collective-permute-done.20.refs_6_), channel_id=1, source_target_pairs={{0,1},{1,2},{2,3},{3,4},{4,5},{5,6},{6,7},{7,8},{8,9},{9,10},{10,1... | collective-permute-start | bytes 589832 | tf_op jit(solution)/shard_map/ppermute | solution.py:208
  77.3 23.3 %collective-permute-start.30 = (bf16[384,256]{1,0:T(8,128)(2,1)}, bf16[384,256]{1,0:T(8,128)(2,1)}, u32[]{:S(2)}, u32[]{:S(2)}) collective-permute-start(bf16[384,256]{1,0:T(8,128)(2,1)} %collective-permute-done.29.refs_5_), channel_id=1, source_target_pairs={{0,15},{1,0},{2,1},{3,2},{4,3},{5,4},{6,5},{7,6},{8,7},{9,8},{10,9... | collective-permute-start | bytes 589832 | tf_op jit(solution)/shard_map/ppermute | solution.py:208
  81.9 5.4 %copy-start.23 = (bf16[384,256]{1,0:T(8,128)(2,1)}, bf16[384,256]{1,0:T(8,128)(2,1)S(1)}, u32[]{:S(2)}) copy-start(bf16[384,256]{1,0:T(8,128)(2,1)S(1)} %collective-permute-done.6.refs_7_) | copy-start | bytes 589828
  81.9 7.3 %collective-permute-start.7 = (bf16[384,256]{1,0:T(8,128)(2,1)S(1)}, bf16[384,256]{1,0:T(8,128)(2,1)}, u32[]{:S(2)}, u32[]{:S(2)}) collective-permute-start(bf16[384,256]{1,0:T(8,128)(2,1)S(1)} %collective-permute-done.6.refs_7_), channel_id=1, source_target_pairs={{0,15},{1,0},{2,1},{3,2},{4,3},{5,4},{6,5},{7,6},{8,7},{9,8},{10,9... | collective-permute-start | bytes 589832 | tf_op jit(solution)/shard_map/ppermute | solution.py:208
  85.3 8.6 %copy-start.3 = (bf16[128,2048]{1,0:T(8,128)(2,1)}, bf16[128,2048]{1,0:T(8,128)(2,1)S(1)}, u32[]{:S(2)}) copy-start(bf16[128,2048]{1,0:T(8,128)(2,1)S(1)} %constant_dynamic-update-slice_fusion.refs_2_) | copy-start | bytes 1572868
  85.4 15.3 %copy-start.24 = (bf16[384,256]{1,0:T(8,128)(2,1)}, bf16[384,256]{1,0:T(8,128)(2,1)S(1)}, u32[]{:S(2)}) copy-start(bf16[384,256]{1,0:T(8,128)(2,1)S(1)} %collective-permute-done.13.refs_8_) | copy-start | bytes 589828
  85.4 25.1 %collective-permute-start.14 = (bf16[384,256]{1,0:T(8,128)(2,1)S(1)}, bf16[384,256]{1,0:T(8,128)(2,1)S(1)}, u32[]{:S(2)}, u32[]{:S(2)}) collective-permute-start(bf16[384,256]{1,0:T(8,128)(2,1)S(1)} %collective-permute-done.13.refs_8_), channel_id=1, source_target_pairs={{0,1},{1,2},{2,3},{3,4},{4,5},{5,6},{6,7},{7,8},{8,9},{9,10},{10,1... | collective-permute-start | bytes 589832 | tf_op jit(solution)/shard_map/ppermute | solution.py:208
  87.3 25.1 %collective-permute-start.22 = (bf16[384,256]{1,0:T(8,128)(2,1)}, bf16[384,256]{1,0:T(8,128)(2,1)}, u32[]{:S(2)}, u32[]{:S(2)}) collective-permute-start(bf16[384,256]{1,0:T(8,128)(2,1)} %collective-permute-done.21.refs_10_), channel_id=1, source_target_pairs={{0,1},{1,2},{2,3},{3,4},{4,5},{5,6},{6,7},{7,8},{8,9},{9,10},{10,1... | collective-permute-start | bytes 589832 | tf_op jit(solution)/shard_map/ppermute | solution.py:208
  89.3 25.1 %collective-permute-start.8 = (bf16[384,256]{1,0:T(8,128)(2,1)}, bf16[384,256]{1,0:T(8,128)(2,1)S(1)}, u32[]{:S(2)}, u32[]{:S(2)}) collective-permute-start(bf16[384,256]{1,0:T(8,128)(2,1)} %collective-permute-done.7.refs_3_), channel_id=1, source_target_pairs={{0,15},{1,0},{2,1},{3,2},{4,3},{5,4},{6,5},{7,6},{8,7},{9,8},{10,9... | collective-permute-start | bytes 589832 | tf_op jit(solution)/shard_map/ppermute | solution.py:208
  100.7 24.8 %collective-permute-start.31 = (bf16[384,256]{1,0:T(8,128)(2,1)}, bf16[384,256]{1,0:T(8,128)(2,1)S(1)}, u32[]{:S(2)}, u32[]{:S(2)}) collective-permute-start(bf16[384,256]{1,0:T(8,128)(2,1)} %collective-permute-done.30.refs_9_), channel_id=1, source_target_pairs={{0,15},{1,0},{2,1},{3,2},{4,3},{5,4},{6,5},{7,6},{8,7},{9,8},{10,9... | collective-permute-start | bytes 589832 | tf_op jit(solution)/shard_map/ppermute | solution.py:208
  110.5 15.0 %copy-start.26 = (bf16[384,256]{1,0:T(8,128)(2,1)}, bf16[384,256]{1,0:T(8,128)(2,1)S(1)}, u32[]{:S(2)}) copy-start(bf16[384,256]{1,0:T(8,128)(2,1)S(1)} %collective-permute-done.14.refs_4_) | copy-start | bytes 589828
  110.5 20.1 %collective-permute-start.15 = (bf16[384,256]{1,0:T(8,128)(2,1)S(1)}, bf16[384,256]{1,0:T(8,128)(2,1)S(1)}, u32[]{:S(2)}, u32[]{:S(2)}) collective-permute-start(bf16[384,256]{1,0:T(8,128)(2,1)S(1)} %collective-permute-done.14.refs_4_), channel_id=1, source_target_pairs={{0,1},{1,2},{2,3},{3,4},{4,5},{5,6},{6,7},{7,8},{8,9},{9,10},{10,1... | collective-permute-start | bytes 589832 | tf_op jit(solution)/shard_map/ppermute | solution.py:208
  112.5 18.2 %collective-permute-start.23 = (bf16[384,256]{1,0:T(8,128)(2,1)}, bf16[384,256]{1,0:T(8,128)(2,1)S(1)}, u32[]{:S(2)}, u32[]{:S(2)}) collective-permute-start(bf16[384,256]{1,0:T(8,128)(2,1)} %collective-permute-done.22.refs_6_), channel_id=1, source_target_pairs={{0,1},{1,2},{2,3},{3,4},{4,5},{5,6},{6,7},{7,8},{8,9},{9,10},{10,1... | collective-permute-start | bytes 589832 | tf_op jit(solution)/shard_map/ppermute | solution.py:208
  114.4 11.1 %copy-start.25 = (bf16[384,256]{1,0:T(8,128)(2,1)}, bf16[384,256]{1,0:T(8,128)(2,1)S(1)}, u32[]{:S(2)}) copy-start(bf16[384,256]{1,0:T(8,128)(2,1)S(1)} %collective-permute-done.8.refs_3_) | copy-start | bytes 589828
  114.4 16.2 %collective-permute-start.24 = (bf16[384,256]{1,0:T(8,128)(2,1)S(1)}, bf16[384,256]{1,0:T(8,128)(2,1)S(1)}, u32[]{:S(2)}, u32[]{:S(2)}) collective-permute-start(bf16[384,256]{1,0:T(8,128)(2,1)S(1)} %collective-permute-done.8.refs_3_), channel_id=1, source_target_pairs={{0,15},{1,0},{2,1},{3,2},{4,3},{5,4},{6,5},{7,6},{8,7},{9,8},{10,9... | collective-permute-start | bytes 589832 | tf_op jit(solution)/shard_map/ppermute | solution.py:208
  130.6 0.7 copy-start.27
  130.6 0.7 copy-start.29
  136.5 27.8 %collective-permute-start.32 = (bf16[384,256]{1,0:T(8,128)(2,1)}, bf16[384,256]{1,0:T(8,128)(2,1)S(1)}, u32[]{:S(2)}, u32[]{:S(2)}) collective-permute-start(bf16[384,256]{1,0:T(8,128)(2,1)} %get-tuple-element.12), channel_id=1, source_target_pairs={{0,16},{1,17},{2,18},{3,19},{4,20},{5,21},{6,22},{7,23},{8,24},{9,... | collective-permute-start | bytes 589832 | tf_op jit(solution)/shard_map/ppermute | solution.py:240
  139.4 24.9 %collective-permute-start.33 = (bf16[192,256]{1,0:T(8,128)(2,1)}, bf16[192,256]{1,0:T(8,128)(2,1)S(1)}, u32[]{:S(2)}, u32[]{:S(2)}) collective-permute-start(bf16[192,256]{1,0:T(8,128)(2,1)} %get-tuple-element.13), channel_id=1, source_target_pairs={{16,80},{64,0},{17,81},{65,1},{18,82},{66,2},{19,83},{67,3},{20,84... | collective-permute-start | bytes 294920 | tf_op jit(solution)/shard_map/ppermute | solution.py:241
  151.9 12.4 %collective-permute-start.34 = (bf16[192,256]{1,0:T(8,128)(2,1)}, bf16[192,256]{1,0:T(8,128)(2,1)S(1)}, u32[]{:S(2)}, u32[]{:S(2)}) collective-permute-start(bf16[192,256]{1,0:T(8,128)(2,1)} %get-tuple-element.14), channel_id=1, source_target_pairs={{16,64},{64,16},{17,65},{65,17},{18,66},{66,18},{19,67},{67,19},{2... | collective-permute-start | bytes 294920 | tf_op jit(solution)/shard_map/ppermute | solution.py:242
  153.8 8.5 %collective-permute-start.35 = (bf16[8,4,256]{2,1,0:T(4,128)(2,1)}, bf16[8,4,256]{2,1,0:T(4,128)(2,1)S(1)}, u32[]{:S(2)}, u32[]{:S(2)}) collective-permute-start(bf16[8,4,256]{2,1,0:T(4,128)(2,1)} %get-tuple-element.15), channel_id=1, source_target_pairs={{0,32},{32,0},{1,33},{33,1},{2,34},{34,2},{3,35},{35,3},{4,36},{36... | collective-permute-start | bytes 49160 | tf_op jit(solution)/shard_map/ppermute | solution.py:243
  158.4 5.9 %collective-permute-start.36 = (bf16[8,4,256]{2,1,0:T(4,128)(2,1)}, bf16[8,4,256]{2,1,0:T(4,128)(2,1)S(1)}, u32[]{:S(2)}, u32[]{:S(2)}) collective-permute-start(bf16[8,4,256]{2,1,0:T(4,128)(2,1)} %get-tuple-element.16), channel_id=1, source_target_pairs={{0,48},{1,49},{2,50},{3,51},{4,52},{5,53},{6,54},{7,55},{8,56},{9,... | collective-permute-start | bytes 49160 | tf_op jit(solution)/shard_map/ppermute | solution.py:249
  162.3 2.0 %copy-start.6 = (bf16[8,4,256]{2,1,0:T(4,128)(2,1)}, bf16[8,4,256]{2,1,0:T(4,128)(2,1)S(1)}, u32[]{:S(2)}) copy-start(bf16[8,4,256]{2,1,0:T(4,128)(2,1)S(1)} %collective-permute-done.35.keep_y_ref) | copy-start | bytes 49156
  164.3 0.7 copy-start.5
  164.3 0.7 copy-start.1
  (4 other events, 2.6 us)

commit v3 on v2

v3 whole, which is shorter than its diff:
```python
import functools

import jax
import jax.numpy as jnp
from jax import lax
from jax.experimental import pallas as pl
from jax.experimental.pallas import tpu as pltpu
from jax.sharding import PartitionSpec as P


stencil_weights = (-205.0 / 72.0, 8.0 / 5.0, -1.0 / 5.0, 8.0 / 315.0, -1.0 / 560.0)
PLANES = 4
VMEM = pl.BlockSpec(memory_space=pltpu.VMEM)


def spread_kernel(own_ref, other_ref, out_ref):
    wide = out_ref.shape[1]
    columns = wide // PLANES
    row = lax.broadcasted_iota(jnp.int32, (2 * wide, 2 * columns), 0) >> 2
    column = lax.broadcasted_iota(jnp.int32, (2 * wide, 2 * columns), 1)
    pick = (row == column).astype(jnp.bfloat16)
    for pair in range(out_ref.shape[0] // 2):
        lanes = slice(2 * columns * pair, 2 * columns * (pair + 1))
        rows = jnp.concatenate([own_ref[:, lanes], other_ref[:, lanes]], axis=0)
        tall = lax.dot_general(
            pick, rows, (((1,), (1,)), ((), ())), preferred_element_type=jnp.float32
        ).astype(jnp.bfloat16)
        out_ref[2 * pair] = tall[:wide]
        out_ref[2 * pair + 1] = tall[wide:]


def spread(own, other):
    bands, total = own.shape
    return pl.pallas_call(
        spread_kernel,
        in_specs=[VMEM, VMEM],
        out_specs=VMEM,
        out_shape=jax.ShapeDtypeStruct((total // 64, 64 * PLANES, 2 * bands), jnp.bfloat16),
        cost_estimate=pl.CostEstimate(flops=5 * 10**8, bytes_accessed=3 * 2**20, transcendentals=0),
        name="spread",
    )(own, other)


def half_of_band():
    return lax.axis_size("band") // 2


def rotate_kernel(first, last, steps, *refs):
    count = len(steps)
    tall_ref = refs[0]
    shards = refs[1 : 1 + count]
    extra_ref, *refs = refs[1 + count :]
    ring = half_of_band()
    index = lax.axis_index("band")
    mine, z = index // ring, index % ring
    sign = 1 - 2 * (lax.axis_index("dx") % 2)
    second = lax.axis_index("dy")
    if last:
        sort_ref, *refs = refs
    _, _, lanes = shards[0].shape
    bands = tall_ref.shape[2]
    plane = lax.broadcasted_iota(jnp.int32, (lanes, bands), 0) & (PLANES - 1)
    masks = [(plane == q).astype(jnp.bfloat16) for q in range(PLANES)]
    left, right = [], []
    for k in range(count):
        origin = lax.rem(z - sign * steps[k] + ring, ring)
        for side in range(2):
            tall = tall_ref[(mine if side == 0 else 1 - mine) * ring + origin]
            left.append(shards[k][side])
            right.append(jnp.concatenate([tall * mask for mask in masks], axis=1))
    total = jnp.dot(
        jnp.concatenate(left, axis=1),
        jnp.concatenate(right, axis=0),
        preferred_element_type=jnp.float32,
    )
    wide = PLANES * bands
    if first:
        out_ref, field_ref, sort_ref = refs
        planes, cells_x, cells_y = extra_ref.shape
        q = lax.broadcasted_iota(jnp.int32, (planes, lanes), 1) & (PLANES - 1)
        cover = (q == lax.broadcasted_iota(jnp.int32, (planes, lanes), 0)).astype(jnp.float32)
        for x in range(cells_x):
            field_ref[x] = lax.dot_general(
                extra_ref[:, x],
                cover,
                (((0,), (0,)), ((), ())),
                precision=lax.Precision.HIGHEST,
                preferred_element_type=jnp.float32,
            )
        i = lax.broadcasted_iota(jnp.int32, (wide, wide), 0)
        j = lax.broadcasted_iota(jnp.int32, (wide, wide), 1)
        shift = bands.bit_length() - 1
        sort_ref[...] = (((i & (bands - 1)) << 2) + (i >> shift) == j).astype(jnp.bfloat16)
        out_ref[...] = total
        return
    total = total + extra_ref[...]
    if not last:
        refs[0][...] = total
        return
    keep_ref, send_ref, keep_x_ref, send_x_ref, keep_y_ref, send_y_ref = refs
    both = jnp.dot(
        total.astype(jnp.bfloat16), sort_ref[...], preferred_element_type=jnp.float32
    ).astype(jnp.bfloat16)
    near, far = both[:, :lanes], both[:, lanes:]
    keep_ref[...] = near
    send_ref[...] = far
    tall = keep_x_ref.shape[0]
    edge = pl.multiple_of(mine * tall, tall)
    keep_x_ref[...] = keep_ref[pl.ds(edge, tall)]
    send_x_ref[...] = send_ref[pl.ds(edge, tall)]
    cells_x = keep_y_ref.shape[0]
    near = near.reshape(cells_x, -1, lanes)
    far = far.reshape(cells_x, -1, lanes)
    cells_y = near.shape[1]

    @pl.when(second == 0)
    def _():
        keep_y_ref[...] = near[:, cells_y - 4 :]
        send_y_ref[...] = far[:, cells_y - 4 :]

    @pl.when(second != 0)
    def _():
        keep_y_ref[...] = near[:, :4]
        send_y_ref[...] = far[:, :4]


def rotate(tall, steps, shards, extra, sort, cells):
    first, last = 0 in steps, sort is not None
    _, points, lanes = shards[0].shape
    wide = PLANES * tall.shape[2]
    total = jax.ShapeDtypeStruct((points, wide), jnp.float32)
    args = [tall, *shards, extra]
    alias = {}
    if first:
        out = [
            total,
            jax.ShapeDtypeStruct((*extra.shape[1:], lanes), jnp.float32),
            jax.ShapeDtypeStruct((wide, wide), jnp.bfloat16),
        ]
    elif last:
        args.append(sort)
        cells_x, cells_y = cells
        half = jax.ShapeDtypeStruct((points, lanes), jnp.bfloat16)
        x_edge = jax.ShapeDtypeStruct((4 * cells_y, lanes), jnp.bfloat16)
        y_edge = jax.ShapeDtypeStruct((cells_x, 4, lanes), jnp.bfloat16)
        out = [half, half, x_edge, x_edge, y_edge, y_edge]
    else:
        alias = {len(args) - 1: 0}
        out = [total]
    return pl.pallas_call(
        functools.partial(rotate_kernel, first, last, tuple(steps)),
        in_specs=[VMEM] * len(args),
        out_specs=[VMEM] * len(out),
        out_shape=out,
        input_output_aliases=alias,
        cost_estimate=pl.CostEstimate(
            flops=4 * 10**8 * len(shards), bytes_accessed=4 * 2**20, transcendentals=0
        ),
        name="rotate",
    )(*args)


def stencil_kernel(
    keep_ref, got_ref, keep_x_ref, send_x_ref, keep_y_ref, send_y_ref, field_ref,
    rotated_ref, out_ref, pad_ref,
):
    cells_x, cells_y, lanes = rotated_ref.shape
    half = cells_x // 2
    rows = slice(8, 8 + cells_y)
    mine = lax.axis_index("band") // half_of_band()
    near, far = half * mine, half * (1 - mine)
    rotated_ref[pl.ds(near, half)] = keep_ref[...]
    rotated_ref[pl.ds(far, half)] = got_ref[...]
    pad_ref[pl.ds(4 + near, half), rows] = keep_ref[...].astype(jnp.float32)
    pad_ref[pl.ds(4 + far, half), rows] = got_ref[...].astype(jnp.float32)
    reach = cells_x + 4
    pad_ref[pl.ds(reach * (1 - mine), 4), rows] = keep_x_ref[...].astype(jnp.float32)
    pad_ref[pl.ds(reach * mine, 4), rows] = send_x_ref[...].astype(jnp.float32)
    keep_y = keep_y_ref[...].astype(jnp.float32)
    send_y = send_y_ref[...].astype(jnp.float32)
    first = lax.axis_index("dy") == 0
    above = slice(8 + cells_y, 12 + cells_y)
    pad_ref[pl.ds(4 + near, half), 4:8] = jnp.where(first, 0.0, keep_y)
    pad_ref[pl.ds(4 + far, half), 4:8] = jnp.where(first, 0.0, send_y)
    pad_ref[pl.ds(4 + near, half), above] = jnp.where(first, keep_y, 0.0)
    pad_ref[pl.ds(4 + far, half), above] = jnp.where(first, send_y, 0.0)
    plane = lax.broadcasted_iota(jnp.int32, (cells_y, lanes), 1) & (PLANES - 1)

    def row(x, carry):
        center = pad_ref[x + 4, rows]
        laplace = 3.0 * stencil_weights[0] * center
        for d in range(1, 5):
            total = pad_ref[x + 4 + d, rows] + pad_ref[x + 4 - d, rows]
            total += pad_ref[x + 4, 8 + d : 8 + d + cells_y] + pad_ref[x + 4, 8 - d : 8 - d + cells_y]
            if d < PLANES:
                total += jnp.where(plane + d < PLANES, pltpu.roll(center, lanes - d, 1), 0.0)
                total += jnp.where(plane >= d, pltpu.roll(center, d, 1), 0.0)
            laplace += stencil_weights[d] * total
        out_ref[x] = (field_ref[x] * center - 0.5 * laplace).astype(jnp.bfloat16)
        return carry

    lax.fori_loop(0, cells_x, row, 0)


def stencil(*arrays):
    half, cells_y, lanes = arrays[0].shape
    cells_x = 2 * half
    out = jax.ShapeDtypeStruct((cells_x, cells_y, lanes), jnp.bfloat16)
    return pl.pallas_call(
        stencil_kernel,
        in_specs=[VMEM] * len(arrays),
        out_specs=[VMEM] * 2,
        out_shape=[out, out],
        scratch_shapes=[pltpu.VMEM((cells_x + 8, cells_y + 16, lanes), jnp.float32)],
        name="stencil",
    )(*arrays)


def groups_of(far):
    return [[0, 1, -1]] + [[d, -d] for d in range(2, far)] + [[far]] if far > 1 else [[0], [1]]


def on_device(orbitals, rotation, potential):
    cells_x, cells_y, lanes = orbitals.shape
    half = cells_x // 2
    points = half * cells_y
    columns = lax.axis_size("band")
    ring = columns // 2
    wide = lax.axis_size("dx")
    mine = lax.axis_index("band") // ring
    across = [(i, (i + ring) % columns) for i in range(columns)]
    hops = {
        turn: [
            (x * columns + i, x * columns + i // ring * ring + (i + turn * (-1) ** x) % ring)
            for x in range(wide)
            for i in range(columns)
        ]
        for turn in (1, -1)
    }

    sent = lax.dynamic_slice_in_dim(orbitals, half * (1 - mine), half, 0)
    kept = lax.dynamic_slice_in_dim(orbitals, half * mine, half, 0)
    came = lax.ppermute(sent, "band", across)
    other = lax.ppermute(rotation, "band", across)
    tall = spread(rotation, other)

    far = ring // 2
    shards = {0: jnp.stack([kept, came]).reshape(2, points, lanes)}
    for distance in range(1, far + 1):
        for turn in (1, -1):
            if distance < far or turn == 1:
                held = shards[turn * (distance - 1)]
                shards[turn * distance] = lax.ppermute(held, ("dx", "band"), hops[turn])

    total = field = sort = None
    for group in groups_of(far):
        last = group == [far]
        out = rotate(
            tall, group, [shards[d] for d in group], potential if total is None else total,
            sort if last else None, (half, cells_y),
        )
        if total is None:
            total, field, sort = out
        elif not last:
            (total,) = out
    keep, send, keep_x, send_x, keep_y, send_y = out

    ends = lax.axis_size("dx") - 1
    near, cross = [], []
    for x in range(ends):
        for i in range(ring):
            low, high = i, ring + i
            near += [(x * columns + high, (x + 1) * columns + high)]
            near += [((x + 1) * columns + low, x * columns + low)]
            cross += [(x * columns + high, (x + 1) * columns + low)]
            cross += [((x + 1) * columns + low, x * columns + high)]
    got = lax.ppermute(send, "band", across)
    keep_x = lax.ppermute(keep_x, ("dx", "band"), near)
    send_x = lax.ppermute(send_x, ("dx", "band"), cross)
    keep_y = lax.ppermute(keep_y, "dy", [(0, 1), (1, 0)])
    turn = [
        (y * columns + i, (1 - y) * columns + (i + ring) % columns)
        for y in range(2)
        for i in range(columns)
    ]
    send_y = lax.ppermute(send_y, ("dy", "band"), turn)
    shape = (half, cells_y, lanes)
    edge = (4, cells_y, lanes)
    rotated, applied = stencil(
        keep.reshape(shape), got.reshape(shape), keep_x.reshape(edge), send_x.reshape(edge),
        keep_y, send_y, field,
    )
    return rotated, applied


def solution(mesh):
    return jax.shard_map(
        on_device,
        mesh=mesh,
        in_specs=(P("dx", "dy", "band"), P("band", None), P(None, "dx", "dy")),
        out_specs=(P("dx", "dy", "band"), P("dx", "dy", "band")),
        check_vma=False,
    )
```

time: 173 us -> 168 us (0.971)
  starting transfers between devices: 128 us -> 90.7 us
  waiting for transfers between devices: 2.01 us -> 33.5 us
  Pallas kernels: 33.5 us -> 37.3 us
    ppermute x32 -> x17, starting transfers between devices: 102 us -> 67.2 us  [the longest x15 60 us: on_device(): shards[turn * distance] = lax.ppermute(held, ('dx', 'band'), hops[turn])]
    ppermute x32 -> x17, waiting for transfers between devices: 0.08 us -> 31.6 us  [the longest x15 28.6 us: on_device(): shards[turn * distance] = lax.ppermute(held, ('dx', 'band'), hops[turn])]
    pallas_call x6 -> x10, Pallas kernels: 33.5 us -> 37.3 us  [the longest x8 29.2 us: rotate(): pl.pallas_call(functools.partial(rotate_kernel, first, last, tuple(steps)...]
    ppermute x1, starting transfers between devices: 12.5 us -> 10.1 us  [on_device(): keep_x = lax.ppermute(keep_x, ('dx', 'band'), near)]
  transfers between devices with their start and end apart: 37 -> 22, of which waited for: 1 -> 9; matrix products, arithmetic and copies ran while one was open for 1% -> 0% of each run, Pallas kernels for 14% -> 17%
where the time goes in v3:
time: 168 us; the launch traced here: 165 us
  starting transfers between devices  90.7 us (54%)
  Pallas kernels  37.3 us (22%)
  waiting for transfers between devices  33.5 us (20%)
  local copies, waits for them, and re-layouts  2.57 us (2%)
    ppermute x15, starting transfers between devices, on_device(): shards[turn * distance] = lax.ppermute(held, ('dx', 'band'), hops[turn])  60 us
    pallas_call x8, Pallas kernels, rotate(): pl.pallas_call(functools.partial(rotate_kernel, first, last, tuple(steps)...  29.2 us
    ppermute x15, waiting for transfers between devices, on_device(): shards[turn * distance] = lax.ppermute(held, ('dx', 'band'), hops[turn])  28.6 us
    ppermute x1, starting transfers between devices, on_device(): keep_x = lax.ppermute(keep_x, ('dx', 'band'), near)  10.1 us
    pallas_call x1, Pallas kernels, stencil(): pl.pallas_call(stencil_kernel, in_specs=[VMEM] * len(arrays), out_specs=[...  4.94 us
    ppermute x1, starting transfers between devices, on_device(): keep_y = lax.ppermute(keep_y, 'dy', [(0, 1), (1, 0)])  4.53 us
    ppermute x1, starting transfers between devices, on_device(): came = lax.ppermute(sent, 'band', across)  4.02 us
    ppermute x1, starting transfers between devices, on_device(): send_y = lax.ppermute(send_y, ('dy', 'band'), turn)  3.96 us
  transfers between devices with their start and end apart: 22, of which 9 were waited for; matrix products, arithmetic and copies ran while one was open for 0% of the time, Pallas kernels for 17%

profile of v3, /device:TPU:1, one launch (start us, length us, event | category | flops | bytes accessed | tf_op | source)
XLA Modules:
  0.0 165.2 jit_solution(14683938009015356151)
XLA Ops:
  0.7 1.1 constant_dynamic-slice_fusion.1
  1.7 4.0 %collective-permute-start.1 = (bf16[8,48,256]{2,1,0:T(8,128)(2,1)S(1)}, bf16[8,48,256]{2,1,0:T(8,128)(2,1)S(1)}, u32[]{:S(2)}, u32[]{:S(2)}) collective-permute-start(bf16[8,48,256]{2,1,0:T(8,128)(2,1)S(1)} %get-tuple-element.21), channel_id=1, source_target_pairs={{0,16},{1,17},{2,18},{3,19},{4,20},{5,21},{6,22},{7,23},{8,24},{9,... | collective-permute-start | bytes 589832 | tf_op jit(solution)/shard_map/ppermute | solution.py:243
  5.7 3.0 %collective-permute-done.1 = bf16[8,48,256]{2,1,0:T(8,128)(2,1)S(1)} collective-permute-done((bf16[8,48,256]{2,1,0:T(8,128)(2,1)S(1)}, bf16[8,48,256]{2,1,0:T(8,128)(2,1)S(1)}, u32[]{:S(2)}, u32[]{:S(2)}) %collective-permute-start.1) | collective-permute-done | bytes 196640 | tf_op jit(solution)/shard_map/ppermute | solution.py:243
  8.8 12.5 %collective-permute-start.2 = (bf16[2,384,256]{2,1,0:T(8,128)(2,1)S(1)}, bf16[2,384,256]{2,1,0:T(8,128)(2,1)S(1)}, u32[]{:S(2)}, u32[]{:S(2)}) collective-permute-start(bf16[2,384,256]{2,1,0:T(8,128)(2,1)S(1)} %pad_maximum_fusion.refs_1_), channel_id=1, source_target_pairs={{0,1},{1,2},{2,3},{3,4},{4,5},{5,6},{6,7},{7,8},{8,9},{9,10},{10,1... | collective-permute-start | bytes 1179656 | tf_op jit(solution)/shard_map/ppermute | solution.py:253
  21.4 1.9 %collective-permute-start.10 = (bf16[2,384,256]{2,1,0:T(8,128)(2,1)S(1)}, bf16[2,384,256]{2,1,0:T(8,128)(2,1)S(1)}, u32[]{:S(2)}, u32[]{:S(2)}) collective-permute-start(bf16[2,384,256]{2,1,0:T(8,128)(2,1)S(1)} %pad_maximum_fusion.refs_1_), channel_id=1, source_target_pairs={{0,15},{1,0},{2,1},{3,2},{4,3},{5,4},{6,5},{7,6},{8,7},{9,8},{10,9... | collective-permute-start | bytes 1179656 | tf_op jit(solution)/shard_map/ppermute | solution.py:253
  23.3 3.1 %collective-permute-done.2.refs_2_ = bf16[2,384,256]{2,1,0:T(8,128)(2,1)S(1)} collective-permute-done((bf16[2,384,256]{2,1,0:T(8,128)(2,1)S(1)}, bf16[2,384,256]{2,1,0:T(8,128)(2,1)S(1)}, u32[]{:S(2)}, u32[]{:S(2)}) %collective-permute-start.2) | collective-permute-done | bytes 393248 | tf_op jit(solution)/shard_map/ppermute | solution.py:253
  26.4 5.3 %collective-permute-start.3 = (bf16[2,384,256]{2,1,0:T(8,128)(2,1)S(1)}, bf16[2,384,256]{2,1,0:T(8,128)(2,1)S(1)}, u32[]{:S(2)}, u32[]{:S(2)}) collective-permute-start(bf16[2,384,256]{2,1,0:T(8,128)(2,1)S(1)} %collective-permute-done.2.refs_2_), channel_id=1, source_target_pairs={{0,1},{1,2},{2,3},{3,4},{4,5},{5,6},{6,7},{7,8},{8,9},{9,10},{10,1... | collective-permute-start | bytes 1179656 | tf_op jit(solution)/shard_map/ppermute | solution.py:253
  31.7 0.8 collective-permute-done.10.refs_3_
  32.5 1.9 %collective-permute-start.11 = (bf16[2,384,256]{2,1,0:T(8,128)(2,1)S(1)}, bf16[2,384,256]{2,1,0:T(8,128)(2,1)S(1)}, u32[]{:S(2)}, u32[]{:S(2)}) collective-permute-start(bf16[2,384,256]{2,1,0:T(8,128)(2,1)S(1)} %collective-permute-done.10.refs_3_), channel_id=1, source_target_pairs={{0,15},{1,0},{2,1},{3,2},{4,3},{5,4},{6,5},{7,6},{8,7},{9,8},{10,9... | collective-permute-start | bytes 1179656 | tf_op jit(solution)/shard_map/ppermute | solution.py:253
  34.4 2.0 %collective-permute-done.3.refs_1_ = bf16[2,384,256]{2,1,0:T(8,128)(2,1)S(1)} collective-permute-done((bf16[2,384,256]{2,1,0:T(8,128)(2,1)S(1)}, bf16[2,384,256]{2,1,0:T(8,128)(2,1)S(1)}, u32[]{:S(2)}, u32[]{:S(2)}) %collective-permute-start.3) | collective-permute-done | bytes 393248 | tf_op jit(solution)/shard_map/ppermute | solution.py:253
  36.4 5.0 %collective-permute-start.4 = (bf16[2,384,256]{2,1,0:T(8,128)(2,1)S(1)}, bf16[2,384,256]{2,1,0:T(8,128)(2,1)S(1)}, u32[]{:S(2)}, u32[]{:S(2)}) collective-permute-start(bf16[2,384,256]{2,1,0:T(8,128)(2,1)S(1)} %collective-permute-done.3.refs_1_), channel_id=1, source_target_pairs={{0,1},{1,2},{2,3},{3,4},{4,5},{5,6},{6,7},{7,8},{8,9},{9,10},{10,1... | collective-permute-start | bytes 1179656 | tf_op jit(solution)/shard_map/ppermute | solution.py:253
  41.4 4.3 %collective-permute-done.11.refs_2_ = bf16[2,384,256]{2,1,0:T(8,128)(2,1)S(1)} collective-permute-done((bf16[2,384,256]{2,1,0:T(8,128)(2,1)S(1)}, bf16[2,384,256]{2,1,0:T(8,128)(2,1)S(1)}, u32[]{:S(2)}, u32[]{:S(2)}) %collective-permute-start.11) | collective-permute-done | bytes 393248 | tf_op jit(solution)/shard_map/ppermute | solution.py:253
  45.7 1.9 %collective-permute-start.12 = (bf16[2,384,256]{2,1,0:T(8,128)(2,1)S(1)}, bf16[2,384,256]{2,1,0:T(8,128)(2,1)S(1)}, u32[]{:S(2)}, u32[]{:S(2)}) collective-permute-start(bf16[2,384,256]{2,1,0:T(8,128)(2,1)S(1)} %collective-permute-done.11.refs_2_), channel_id=1, source_target_pairs={{0,15},{1,0},{2,1},{3,2},{4,3},{5,4},{6,5},{7,6},{8,7},{9,8},{10,9... | collective-permute-start | bytes 1179656 | tf_op jit(solution)/shard_map/ppermute | solution.py:253
  47.6 0.0 collective-permute-done.4.refs_1_
  47.6 4.9 %collective-permute-start.5 = (bf16[2,384,256]{2,1,0:T(8,128)(2,1)S(1)}, bf16[2,384,256]{2,1,0:T(8,128)(2,1)S(1)}, u32[]{:S(2)}, u32[]{:S(2)}) collective-permute-start(bf16[2,384,256]{2,1,0:T(8,128)(2,1)S(1)} %collective-permute-done.4.refs_1_), channel_id=1, source_target_pairs={{0,1},{1,2},{2,3},{3,4},{4,5},{5,6},{6,7},{7,8},{8,9},{9,10},{10,1... | collective-permute-start | bytes 1179656 | tf_op jit(solution)/shard_map/ppermute | solution.py:253
  52.5 7.0 %collective-permute-done.12.refs_2_ = bf16[2,384,256]{2,1,0:T(8,128)(2,1)S(1)} collective-permute-done((bf16[2,384,256]{2,1,0:T(8,128)(2,1)S(1)}, bf16[2,384,256]{2,1,0:T(8,128)(2,1)S(1)}, u32[]{:S(2)}, u32[]{:S(2)}) %collective-permute-start.12) | collective-permute-done | bytes 393248 | tf_op jit(solution)/shard_map/ppermute | solution.py:253
  59.5 1.9 %collective-permute-start.13 = (bf16[2,384,256]{2,1,0:T(8,128)(2,1)S(1)}, bf16[2,384,256]{2,1,0:T(8,128)(2,1)S(1)}, u32[]{:S(2)}, u32[]{:S(2)}) collective-permute-start(bf16[2,384,256]{2,1,0:T(8,128)(2,1)S(1)} %collective-permute-done.12.refs_2_), channel_id=1, source_target_pairs={{0,15},{1,0},{2,1},{3,2},{4,3},{5,4},{6,5},{7,6},{8,7},{9,8},{10,9... | collective-permute-start | bytes 1179656 | tf_op jit(solution)/shard_map/ppermute | solution.py:253
  61.4 0.0 collective-permute-done.5.refs_1_
  61.4 0.0 copy-start.4
  61.4 4.9 %collective-permute-start.6 = (bf16[2,384,256]{2,1,0:T(8,128)(2,1)S(1)}, bf16[2,384,256]{2,1,0:T(8,128)(2,1)S(1)}, u32[]{:S(2)}, u32[]{:S(2)}) collective-permute-start(bf16[2,384,256]{2,1,0:T(8,128)(2,1)S(1)} %collective-permute-done.5.refs_1_), channel_id=1, source_target_pairs={{0,1},{1,2},{2,3},{3,4},{4,5},{5,6},{6,7},{7,8},{8,9},{9,10},{10,1... | collective-permute-start | bytes 1179656 | tf_op jit(solution)/shard_map/ppermute | solution.py:253
  66.3 6.1 %collective-permute-done.13.refs_2_ = bf16[2,384,256]{2,1,0:T(8,128)(2,1)S(1)} collective-permute-done((bf16[2,384,256]{2,1,0:T(8,128)(2,1)S(1)}, bf16[2,384,256]{2,1,0:T(8,128)(2,1)S(1)}, u32[]{:S(2)}, u32[]{:S(2)}) %collective-permute-start.13) | collective-permute-done | bytes 393248 | tf_op jit(solution)/shard_map/ppermute | solution.py:253
  72.4 1.9 %collective-permute-start.14 = (bf16[2,384,256]{2,1,0:T(8,128)(2,1)S(1)}, bf16[2,384,256]{2,1,0:T(8,128)(2,1)S(1)}, u32[]{:S(2)}, u32[]{:S(2)}) collective-permute-start(bf16[2,384,256]{2,1,0:T(8,128)(2,1)S(1)} %collective-permute-done.13.refs_2_), channel_id=1, source_target_pairs={{0,15},{1,0},{2,1},{3,2},{4,3},{5,4},{6,5},{7,6},{8,7},{9,8},{10,9... | collective-permute-start | bytes 1179656 | tf_op jit(solution)/shard_map/ppermute | solution.py:253
  74.3 0.0 collective-permute-done.6.refs_1_
  74.4 0.0 copy-start.6
  74.4 4.9 %collective-permute-start.7 = (bf16[2,384,256]{2,1,0:T(8,128)(2,1)S(1)}, bf16[2,384,256]{2,1,0:T(8,128)(2,1)S(1)}, u32[]{:S(2)}, u32[]{:S(2)}) collective-permute-start(bf16[2,384,256]{2,1,0:T(8,128)(2,1)S(1)} %collective-permute-done.6.refs_1_), channel_id=1, source_target_pairs={{0,1},{1,2},{2,3},{3,4},{4,5},{5,6},{6,7},{7,8},{8,9},{9,10},{10,1... | collective-permute-start | bytes 1179656 | tf_op jit(solution)/shard_map/ppermute | solution.py:253
  79.2 5.3 %collective-permute-done.14.refs_2_ = bf16[2,384,256]{2,1,0:T(8,128)(2,1)S(1)} collective-permute-done((bf16[2,384,256]{2,1,0:T(8,128)(2,1)S(1)}, bf16[2,384,256]{2,1,0:T(8,128)(2,1)S(1)}, u32[]{:S(2)}, u32[]{:S(2)}) %collective-permute-start.14) | collective-permute-done | bytes 393248 | tf_op jit(solution)/shard_map/ppermute | solution.py:253
  84.5 1.9 %collective-permute-start.15 = (bf16[2,384,256]{2,1,0:T(8,128)(2,1)S(1)}, bf16[2,384,256]{2,1,0:T(8,128)(2,1)}, u32[]{:S(2)}, u32[]{:S(2)}) collective-permute-start(bf16[2,384,256]{2,1,0:T(8,128)(2,1)S(1)} %collective-permute-done.14.refs_2_), channel_id=1, source_target_pairs={{0,15},{1,0},{2,1},{3,2},{4,3},{5,4},{6,5},{7,6},{8,7},{9,8},{10,9... | collective-permute-start | bytes 1179656 | tf_op jit(solution)/shard_map/ppermute | solution.py:253
  86.4 3.2 %collective-permute-start = (bf16[64,2048]{1,0:T(8,128)(2,1)}, bf16[64,2048]{1,0:T(8,128)(2,1)}, u32[]{:S(2)}, u32[]{:S(2)}) collective-permute-start(bf16[64,2048]{1,0:T(8,128)(2,1)} %own_ref.1), channel_id=1, source_target_pairs={{0,16},{1,17},{2,18},{3,19},{4,20},{5,21},{6,22},{7,23},{8,24},{9,... | collective-permute-start | bytes 786440 | tf_op jit(solution)/shard_map/ppermute | solution.py:244
  89.7 0.0 collective-permute-done.7.refs_1_
  89.7 0.0 copy-start.8
  89.7 4.6 %collective-permute-start.8 = (bf16[2,384,256]{2,1,0:T(8,128)(2,1)S(1)}, bf16[2,384,256]{2,1,0:T(8,128)(2,1)}, u32[]{:S(2)}, u32[]{:S(2)}) collective-permute-start(bf16[2,384,256]{2,1,0:T(8,128)(2,1)S(1)} %collective-permute-done.7.refs_1_), channel_id=1, source_target_pairs={{0,1},{1,2},{2,3},{3,4},{4,5},{5,6},{6,7},{7,8},{8,9},{9,10},{10,1... | collective-permute-start | bytes 1179656 | tf_op jit(solution)/shard_map/ppermute | solution.py:253
  94.3 0.0 copy-done.16
  94.3 0.0 collective-permute-done.other_ref
  94.3 3.1 %spread.1.refs_0_ = bf16[32,256,128]{2,1,0:T(8,128)(2,1)} custom-call(bf16[64,2048]{1,0:T(8,128)(2,1)} %own_ref.1, bf16[64,2048]{1,0:T(8,128)(2,1)} %collective-permute-done.other_ref), custom_call_target="tpu_custom_call" | custom-call | flops 500000000 | bytes 3145728 | tf_op jit(solution)/shard_map/spread/pallas_call | solution.py:34
  97.4 0.0 collective-permute-done.15.refs_2_
  97.4 1.9 %collective-permute-start.16 = (bf16[2,384,256]{2,1,0:T(8,128)(2,1)}, bf16[2,384,256]{2,1,0:T(8,128)(2,1)}, u32[]{:S(2)}, u32[]{:S(2)}) collective-permute-start(bf16[2,384,256]{2,1,0:T(8,128)(2,1)} %collective-permute-done.15.refs_2_), channel_id=1, source_target_pairs={{0,15},{1,0},{2,1},{3,2},{4,3},{5,4},{6,5},{7,6},{8,7},{9,8},{10,9... | collective-permute-start | bytes 1179656 | tf_op jit(solution)/shard_map/ppermute | solution.py:253
  99.3 4.5 %rotate.8 = (f32[384,512]{1,0:T(8,128)}, f32[16,48,256]{2,1,0:T(8,128)}, bf16[512,512]{1,0:T(8,128)(2,1)}) custom-call(bf16[32,256,128]{2,1,0:T(8,128)(2,1)} %spread.1.refs_0_, bf16[2,384,256]{2,1,0:T(8,128)(2,1)} %copy-done.10, bf16[2,384,256]{2,1,0:T(8,128)(2,1)} %copy-done.16, bf16[2,384,256]{2,1,0:T(8,128)(2,1)} %copy-done.17, f32[4,16,48]{2,1,0:T(8,128)} %refs_4_.1), custom_call_target="tpu_custom_call" | custom-call | flops 1200000000 | bytes 4194304 | tf_op jit(solution)/shard_map/rotate/pallas_call | solution.py:150
  103.9 0.0 collective-permute-done.8.refs_1_
  103.9 4.6 %collective-permute-start.9 = (bf16[2,384,256]{2,1,0:T(8,128)(2,1)}, bf16[2,384,256]{2,1,0:T(8,128)(2,1)S(1)}, u32[]{:S(2)}, u32[]{:S(2)}) collective-permute-start(bf16[2,384,256]{2,1,0:T(8,128)(2,1)} %collective-permute-done.8.refs_1_), channel_id=1, source_target_pairs={{0,1},{1,2},{2,3},{3,4},{4,5},{5,6},{6,7},{7,8},{8,9},{9,10},{10,1... | collective-permute-start | bytes 1179656 | tf_op jit(solution)/shard_map/ppermute | solution.py:253
  108.6 3.5 %rotate.9.refs_3_ = f32[384,512]{1,0:T(8,128)} custom-call(bf16[32,256,128]{2,1,0:T(8,128)(2,1)} %spread.1.refs_0_, bf16[2,384,256]{2,1,0:T(8,128)(2,1)} %copy-done, bf16[2,384,256]{2,1,0:T(8,128)(2,1)} %copy-done.1, f32[384,512]{1,0:T(8,128)} %get-tuple-element.11.refs_3_), custom_call_target="tpu_custom_call", output_to_operand_aliasing={{}: (3, {})} | custom-call | flops 800000000 | bytes 4194304 | tf_op jit(solution)/shard_map/rotate/pallas_call | solution.py:150
  112.1 3.5 %rotate.10.refs_3_ = f32[384,512]{1,0:T(8,128)} custom-call(bf16[32,256,128]{2,1,0:T(8,128)(2,1)} %spread.1.refs_0_, bf16[2,384,256]{2,1,0:T(8,128)(2,1)} %copy-done.2, bf16[2,384,256]{2,1,0:T(8,128)(2,1)} %copy-done.3, f32[384,512]{1,0:T(8,128)} %rotate.9.refs_3_), custom_call_target="tpu_custom_call", output_to_operand_aliasing={{}: (3, {})} | custom-call | flops 800000000 | bytes 4194304 | tf_op jit(solution)/shard_map/rotate/pallas_call | solution.py:150
  115.6 3.5 %rotate.11.refs_3_ = f32[384,512]{1,0:T(8,128)} custom-call(bf16[32,256,128]{2,1,0:T(8,128)(2,1)} %spread.1.refs_0_, bf16[2,384,256]{2,1,0:T(8,128)(2,1)} %copy-done.4, bf16[2,384,256]{2,1,0:T(8,128)(2,1)} %copy-done.5, f32[384,512]{1,0:T(8,128)} %rotate.10.refs_3_), custom_call_target="tpu_custom_call", output_to_operand_aliasing={{}: (3, {})} | custom-call | flops 800000000 | bytes 4194304 | tf_op jit(solution)/shard_map/rotate/pallas_call | solution.py:150
  119.2 3.5 %rotate.12.refs_3_ = f32[384,512]{1,0:T(8,128)} custom-call(bf16[32,256,128]{2,1,0:T(8,128)(2,1)} %spread.1.refs_0_, bf16[2,384,256]{2,1,0:T(8,128)(2,1)} %copy-done.6, bf16[2,384,256]{2,1,0:T(8,128)(2,1)} %copy-done.7, f32[384,512]{1,0:T(8,128)} %rotate.11.refs_3_), custom_call_target="tpu_custom_call", output_to_operand_aliasing={{}: (3, {})} | custom-call | flops 800000000 | bytes 4194304 | tf_op jit(solution)/shard_map/rotate/pallas_call | solution.py:150
  122.7 3.5 %rotate.13.refs_3_ = f32[384,512]{1,0:T(8,128)} custom-call(bf16[32,256,128]{2,1,0:T(8,128)(2,1)} %spread.1.refs_0_, bf16[2,384,256]{2,1,0:T(8,128)(2,1)} %copy-done.8, bf16[2,384,256]{2,1,0:T(8,128)(2,1)} %collective-permute-done.15.refs_2_, f32[384,512]{1,0:T(8,128)} %rotate.12.refs_3_), custom_call_target="tpu_custom_call", output_to_operand_aliasing={{}: (3, {})} | custom-call | flops 800000000 | bytes 4194304 | tf_op jit(solution)/shard_map/rotate/pallas_call | solution.py:150
  126.2 0.0 collective-permute-done.16.refs_2_
  126.2 3.5 %rotate.14.refs_2_ = f32[384,512]{1,0:T(8,128)} custom-call(bf16[32,256,128]{2,1,0:T(8,128)(2,1)} %spread.1.refs_0_, bf16[2,384,256]{2,1,0:T(8,128)(2,1)} %collective-permute-done.8.refs_1_, bf16[2,384,256]{2,1,0:T(8,128)(2,1)} %collective-permute-done.16.refs_2_, f32[384,512]{1,0:T(8,128)} %rotate.13.refs_3_), custom_call_target="tpu_custom_call", output_to_operand_aliasing={{}: (3, {})} | custom-call | flops 800000000 | bytes 4194304 | tf_op jit(solution)/shard_map/rotate/pallas_call | solution.py:150
  129.8 0.0 collective-permute-done.9.refs_1_
  129.8 0.7 copy-done.9
  130.5 3.5 %rotate.15 = (bf16[384,256]{1,0:T(8,128)(2,1)}, bf16[384,256]{1,0:T(8,128)(2,1)}, bf16[192,256]{1,0:T(8,128)(2,1)}, bf16[192,256]{1,0:T(8,128)(2,1)}, bf16[8,4,2...) custom-call(bf16[32,256,128]{2,1,0:T(8,128)(2,1)} %spread.1.refs_0_, bf16[2,384,256]{2,1,0:T(8,128)(2,1)} %copy-done.9, ...), custom_call_target="tpu_custom_call" | custom-call | flops 400000000 | bytes 4194304 | tf_op jit(solution)/shard_map/rotate/pallas_call | solution.py:150
  134.0 3.0 %collective-permute-start.17 = (bf16[384,256]{1,0:T(8,128)(2,1)}, bf16[384,256]{1,0:T(8,128)(2,1)S(1)}, u32[]{:S(2)}, u32[]{:S(2)}) collective-permute-start(bf16[384,256]{1,0:T(8,128)(2,1)} %get-tuple-element.14), channel_id=1, source_target_pairs={{0,16},{1,17},{2,18},{3,19},{4,20},{5,21},{6,22},{7,23},{8,24},{9,... | collective-permute-start | bytes 589832 | tf_op jit(solution)/shard_map/ppermute | solution.py:277
  137.1 10.1 %collective-permute-start.18 = (bf16[192,256]{1,0:T(8,128)(2,1)}, bf16[192,256]{1,0:T(8,128)(2,1)S(1)}, u32[]{:S(2)}, u32[]{:S(2)}) collective-permute-start(bf16[192,256]{1,0:T(8,128)(2,1)} %get-tuple-element.15), channel_id=1, source_target_pairs={{16,80},{64,0},{17,81},{65,1},{18,82},{66,2},{19,83},{67,3},{20,84... | collective-permute-start | bytes 294920 | tf_op jit(solution)/shard_map/ppermute | solution.py:278
  147.2 1.9 %collective-permute-start.19 = (bf16[192,256]{1,0:T(8,128)(2,1)}, bf16[192,256]{1,0:T(8,128)(2,1)S(1)}, u32[]{:S(2)}, u32[]{:S(2)}) collective-permute-start(bf16[192,256]{1,0:T(8,128)(2,1)} %get-tuple-element.16), channel_id=1, source_target_pairs={{16,64},{64,16},{17,65},{65,17},{18,66},{66,18},{19,67},{67,19},{2... | collective-permute-start | bytes 294920 | tf_op jit(solution)/shard_map/ppermute | solution.py:279
  149.1 4.5 %collective-permute-start.20 = (bf16[8,4,256]{2,1,0:T(4,128)(2,1)}, bf16[8,4,256]{2,1,0:T(4,128)(2,1)S(1)}, u32[]{:S(2)}, u32[]{:S(2)}) collective-permute-start(bf16[8,4,256]{2,1,0:T(4,128)(2,1)} %get-tuple-element.17), channel_id=1, source_target_pairs={{0,32},{32,0},{1,33},{33,1},{2,34},{34,2},{3,35},{35,3},{4,36},{36... | collective-permute-start | bytes 49160 | tf_op jit(solution)/shard_map/ppermute | solution.py:280
  153.6 4.0 %collective-permute-start.21 = (bf16[8,4,256]{2,1,0:T(4,128)(2,1)}, bf16[8,4,256]{2,1,0:T(4,128)(2,1)S(1)}, u32[]{:S(2)}, u32[]{:S(2)}) collective-permute-start(bf16[8,4,256]{2,1,0:T(4,128)(2,1)} %get-tuple-element.18), channel_id=1, source_target_pairs={{0,48},{1,49},{2,50},{3,51},{4,52},{5,53},{6,54},{7,55},{8,56},{9,... | collective-permute-start | bytes 49160 | tf_op jit(solution)/shard_map/ppermute | solution.py:286
  157.6 0.0 collective-permute-done.20.keep_y_ref
  157.6 1.9 %collective-permute-done.21.send_y_ref = bf16[8,4,256]{2,1,0:T(4,128)(2,1)S(1)} collective-permute-done((bf16[8,4,256]{2,1,0:T(4,128)(2,1)}, bf16[8,4,256]{2,1,0:T(4,128)(2,1)S(1)}, u32[]{:S(2)}, u32[]{:S(2)}) %collective-permute-start.21) | collective-permute-done | bytes 16416 | tf_op jit(solution)/shard_map/ppermute | solution.py:286
  159.5 0.0 collective-permute-done.18
  159.5 0.0 collective-permute-done.19
  159.5 0.0 collective-permute-done.17
  159.6 0.5 copy-done.15
  160.1 0.1 copy-done.12
  160.2 0.0 copy-done.13
  160.2 0.1 copy-done.11
  160.3 4.9 %stencil.1 = (bf16[16,48,256]{2,1,0:T(8,128)(2,1)}, bf16[16,48,256]{2,1,0:T(8,128)(2,1)}) custom-call(bf16[8,48,256]{2,1,0:T(8,128)(2,1)} %bitcast.8, bf16[8,48,256]{2,1,0:T(8,128)(2,1)} %bitcast.9, bf16[4,48,256]{2,1,0:T(8,128)(2,1)} %bitcast.10, bf16[4,48,256]{2,1,0:T(8,128)(2,1)} %bitcast.11, bf16[8,4,256]{2,1,0:T(4,128)(2,1)} %copy-done.14, ...), custom_call_target="tpu_custom_call" | custom-call | tf_op jit(solution)/shard_map/stencil/pallas_call | solution.py:209
  (28 shorter events, 0.1 us)
Async XLA Ops:
  1.7 7.1 %collective-permute-start.1 = (bf16[8,48,256]{2,1,0:T(8,128)(2,1)S(1)}, bf16[8,48,256]{2,1,0:T(8,128)(2,1)S(1)}, u32[]{:S(2)}, u32[]{:S(2)}) collective-permute-start(bf16[8,48,256]{2,1,0:T(8,128)(2,1)S(1)} %get-tuple-element.21), channel_id=1, source_target_pairs={{0,16},{1,17},{2,18},{3,19},{4,20},{5,21},{6,22},{7,23},{8,24},{9,... | collective-permute-start | bytes 589832 | tf_op jit(solution)/shard_map/ppermute | solution.py:243
  8.8 80.8 %copy-start.10 = (bf16[2,384,256]{2,1,0:T(8,128)(2,1)}, bf16[2,384,256]{2,1,0:T(8,128)(2,1)S(1)}, u32[]{:S(2)}) copy-start(bf16[2,384,256]{2,1,0:T(8,128)(2,1)S(1)} %pad_maximum_fusion.refs_1_) | copy-start | bytes 1179652
  8.8 17.5 %collective-permute-start.2 = (bf16[2,384,256]{2,1,0:T(8,128)(2,1)S(1)}, bf16[2,384,256]{2,1,0:T(8,128)(2,1)S(1)}, u32[]{:S(2)}, u32[]{:S(2)}) collective-permute-start(bf16[2,384,256]{2,1,0:T(8,128)(2,1)S(1)} %pad_maximum_fusion.refs_1_), channel_id=1, source_target_pairs={{0,1},{1,2},{2,3},{3,4},{4,5},{5,6},{6,7},{7,8},{8,9},{9,10},{10,1... | collective-permute-start | bytes 1179656 | tf_op jit(solution)/shard_map/ppermute | solution.py:253
  21.4 11.1 %collective-permute-start.10 = (bf16[2,384,256]{2,1,0:T(8,128)(2,1)S(1)}, bf16[2,384,256]{2,1,0:T(8,128)(2,1)S(1)}, u32[]{:S(2)}, u32[]{:S(2)}) collective-permute-start(bf16[2,384,256]{2,1,0:T(8,128)(2,1)S(1)} %pad_maximum_fusion.refs_1_), channel_id=1, source_target_pairs={{0,15},{1,0},{2,1},{3,2},{4,3},{5,4},{6,5},{7,6},{8,7},{9,8},{10,9... | collective-permute-start | bytes 1179656 | tf_op jit(solution)/shard_map/ppermute | solution.py:253
  26.4 67.9 %copy-start.16 = (bf16[2,384,256]{2,1,0:T(8,128)(2,1)}, bf16[2,384,256]{2,1,0:T(8,128)(2,1)S(1)}, u32[]{:S(2)}) copy-start(bf16[2,384,256]{2,1,0:T(8,128)(2,1)S(1)} %collective-permute-done.2.refs_2_) | copy-start | bytes 1179652
  26.4 10.0 %collective-permute-start.3 = (bf16[2,384,256]{2,1,0:T(8,128)(2,1)S(1)}, bf16[2,384,256]{2,1,0:T(8,128)(2,1)S(1)}, u32[]{:S(2)}, u32[]{:S(2)}) collective-permute-start(bf16[2,384,256]{2,1,0:T(8,128)(2,1)S(1)} %collective-permute-done.2.refs_2_), channel_id=1, source_target_pairs={{0,1},{1,2},{2,3},{3,4},{4,5},{5,6},{6,7},{7,8},{8,9},{9,10},{10,1... | collective-permute-start | bytes 1179656 | tf_op jit(solution)/shard_map/ppermute | solution.py:253
  32.5 61.8 %copy-start.17 = (bf16[2,384,256]{2,1,0:T(8,128)(2,1)}, bf16[2,384,256]{2,1,0:T(8,128)(2,1)S(1)}, u32[]{:S(2)}) copy-start(bf16[2,384,256]{2,1,0:T(8,128)(2,1)S(1)} %collective-permute-done.10.refs_3_) | copy-start | bytes 1179652
  32.5 13.2 %collective-permute-start.11 = (bf16[2,384,256]{2,1,0:T(8,128)(2,1)S(1)}, bf16[2,384,256]{2,1,0:T(8,128)(2,1)S(1)}, u32[]{:S(2)}, u32[]{:S(2)}) collective-permute-start(bf16[2,384,256]{2,1,0:T(8,128)(2,1)S(1)} %collective-permute-done.10.refs_3_), channel_id=1, source_target_pairs={{0,15},{1,0},{2,1},{3,2},{4,3},{5,4},{6,5},{7,6},{8,7},{9,8},{10,9... | collective-permute-start | bytes 1179656 | tf_op jit(solution)/shard_map/ppermute | solution.py:253
  36.4 67.4 %copy-start = (bf16[2,384,256]{2,1,0:T(8,128)(2,1)}, bf16[2,384,256]{2,1,0:T(8,128)(2,1)S(1)}, u32[]{:S(2)}) copy-start(bf16[2,384,256]{2,1,0:T(8,128)(2,1)S(1)} %collective-permute-done.3.refs_1_) | copy-start | bytes 1179652
  36.4 11.2 %collective-permute-start.4 = (bf16[2,384,256]{2,1,0:T(8,128)(2,1)S(1)}, bf16[2,384,256]{2,1,0:T(8,128)(2,1)S(1)}, u32[]{:S(2)}, u32[]{:S(2)}) collective-permute-start(bf16[2,384,256]{2,1,0:T(8,128)(2,1)S(1)} %collective-permute-done.3.refs_1_), channel_id=1, source_target_pairs={{0,1},{1,2},{2,3},{3,4},{4,5},{5,6},{6,7},{7,8},{8,9},{9,10},{10,1... | collective-permute-start | bytes 1179656 | tf_op jit(solution)/shard_map/ppermute | solution.py:253
  45.7 58.2 %copy-start.1 = (bf16[2,384,256]{2,1,0:T(8,128)(2,1)}, bf16[2,384,256]{2,1,0:T(8,128)(2,1)S(1)}, u32[]{:S(2)}) copy-start(bf16[2,384,256]{2,1,0:T(8,128)(2,1)S(1)} %collective-permute-done.11.refs_2_) | copy-start | bytes 1179652
  45.7 13.8 %collective-permute-start.12 = (bf16[2,384,256]{2,1,0:T(8,128)(2,1)S(1)}, bf16[2,384,256]{2,1,0:T(8,128)(2,1)S(1)}, u32[]{:S(2)}, u32[]{:S(2)}) collective-permute-start(bf16[2,384,256]{2,1,0:T(8,128)(2,1)S(1)} %collective-permute-done.11.refs_2_), channel_id=1, source_target_pairs={{0,15},{1,0},{2,1},{3,2},{4,3},{5,4},{6,5},{7,6},{8,7},{9,8},{10,9... | collective-permute-start | bytes 1179656 | tf_op jit(solution)/shard_map/ppermute | solution.py:253
  47.6 56.2 %copy-start.2 = (bf16[2,384,256]{2,1,0:T(8,128)(2,1)}, bf16[2,384,256]{2,1,0:T(8,128)(2,1)S(1)}, u32[]{:S(2)}) copy-start(bf16[2,384,256]{2,1,0:T(8,128)(2,1)S(1)} %collective-permute-done.4.refs_1_) | copy-start | bytes 1179652
  47.6 13.8 %collective-permute-start.5 = (bf16[2,384,256]{2,1,0:T(8,128)(2,1)S(1)}, bf16[2,384,256]{2,1,0:T(8,128)(2,1)S(1)}, u32[]{:S(2)}, u32[]{:S(2)}) collective-permute-start(bf16[2,384,256]{2,1,0:T(8,128)(2,1)S(1)} %collective-permute-done.4.refs_1_), channel_id=1, source_target_pairs={{0,1},{1,2},{2,3},{3,4},{4,5},{5,6},{6,7},{7,8},{8,9},{9,10},{10,1... | collective-permute-start | bytes 1179656 | tf_op jit(solution)/shard_map/ppermute | solution.py:253
  59.5 44.4 %copy-start.3 = (bf16[2,384,256]{2,1,0:T(8,128)(2,1)}, bf16[2,384,256]{2,1,0:T(8,128)(2,1)S(1)}, u32[]{:S(2)}) copy-start(bf16[2,384,256]{2,1,0:T(8,128)(2,1)S(1)} %collective-permute-done.12.refs_2_) | copy-start | bytes 1179652
  59.5 12.9 %collective-permute-start.13 = (bf16[2,384,256]{2,1,0:T(8,128)(2,1)S(1)}, bf16[2,384,256]{2,1,0:T(8,128)(2,1)S(1)}, u32[]{:S(2)}, u32[]{:S(2)}) collective-permute-start(bf16[2,384,256]{2,1,0:T(8,128)(2,1)S(1)} %collective-permute-done.12.refs_2_), channel_id=1, source_target_pairs={{0,15},{1,0},{2,1},{3,2},{4,3},{5,4},{6,5},{7,6},{8,7},{9,8},{10,9... | collective-permute-start | bytes 1179656 | tf_op jit(solution)/shard_map/ppermute | solution.py:253
  61.4 42.5 %copy-start.4 = (bf16[2,384,256]{2,1,0:T(8,128)(2,1)}, bf16[2,384,256]{2,1,0:T(8,128)(2,1)S(1)}, u32[]{:S(2)}) copy-start(bf16[2,384,256]{2,1,0:T(8,128)(2,1)S(1)} %collective-permute-done.5.refs_1_) | copy-start | bytes 1179652
  61.4 12.9 %collective-permute-start.6 = (bf16[2,384,256]{2,1,0:T(8,128)(2,1)S(1)}, bf16[2,384,256]{2,1,0:T(8,128)(2,1)S(1)}, u32[]{:S(2)}, u32[]{:S(2)}) collective-permute-start(bf16[2,384,256]{2,1,0:T(8,128)(2,1)S(1)} %collective-permute-done.5.refs_1_), channel_id=1, source_target_pairs={{0,1},{1,2},{2,3},{3,4},{4,5},{5,6},{6,7},{7,8},{8,9},{9,10},{10,1... | collective-permute-start | bytes 1179656 | tf_op jit(solution)/shard_map/ppermute | solution.py:253
  72.4 31.4 %copy-start.5 = (bf16[2,384,256]{2,1,0:T(8,128)(2,1)}, bf16[2,384,256]{2,1,0:T(8,128)(2,1)S(1)}, u32[]{:S(2)}) copy-start(bf16[2,384,256]{2,1,0:T(8,128)(2,1)S(1)} %collective-permute-done.13.refs_2_) | copy-start | bytes 1179652
  72.4 12.1 %collective-permute-start.14 = (bf16[2,384,256]{2,1,0:T(8,128)(2,1)S(1)}, bf16[2,384,256]{2,1,0:T(8,128)(2,1)S(1)}, u32[]{:S(2)}, u32[]{:S(2)}) collective-permute-start(bf16[2,384,256]{2,1,0:T(8,128)(2,1)S(1)} %collective-permute-done.13.refs_2_), channel_id=1, source_target_pairs={{0,15},{1,0},{2,1},{3,2},{4,3},{5,4},{6,5},{7,6},{8,7},{9,8},{10,9... | collective-permute-start | bytes 1179656 | tf_op jit(solution)/shard_map/ppermute | solution.py:253
  74.4 29.5 %copy-start.6 = (bf16[2,384,256]{2,1,0:T(8,128)(2,1)}, bf16[2,384,256]{2,1,0:T(8,128)(2,1)S(1)}, u32[]{:S(2)}) copy-start(bf16[2,384,256]{2,1,0:T(8,128)(2,1)S(1)} %collective-permute-done.6.refs_1_) | copy-start | bytes 1179652
  74.4 15.3 %collective-permute-start.7 = (bf16[2,384,256]{2,1,0:T(8,128)(2,1)S(1)}, bf16[2,384,256]{2,1,0:T(8,128)(2,1)S(1)}, u32[]{:S(2)}, u32[]{:S(2)}) collective-permute-start(bf16[2,384,256]{2,1,0:T(8,128)(2,1)S(1)} %collective-permute-done.6.refs_1_), channel_id=1, source_target_pairs={{0,1},{1,2},{2,3},{3,4},{4,5},{5,6},{6,7},{7,8},{8,9},{9,10},{10,1... | collective-permute-start | bytes 1179656 | tf_op jit(solution)/shard_map/ppermute | solution.py:253
  84.5 19.4 %copy-start.7 = (bf16[2,384,256]{2,1,0:T(8,128)(2,1)}, bf16[2,384,256]{2,1,0:T(8,128)(2,1)S(1)}, u32[]{:S(2)}) copy-start(bf16[2,384,256]{2,1,0:T(8,128)(2,1)S(1)} %collective-permute-done.14.refs_2_) | copy-start | bytes 1179652
  84.5 12.9 %collective-permute-start.15 = (bf16[2,384,256]{2,1,0:T(8,128)(2,1)S(1)}, bf16[2,384,256]{2,1,0:T(8,128)(2,1)}, u32[]{:S(2)}, u32[]{:S(2)}) collective-permute-start(bf16[2,384,256]{2,1,0:T(8,128)(2,1)S(1)} %collective-permute-done.14.refs_2_), channel_id=1, source_target_pairs={{0,15},{1,0},{2,1},{3,2},{4,3},{5,4},{6,5},{7,6},{8,7},{9,8},{10,9... | collective-permute-start | bytes 1179656 | tf_op jit(solution)/shard_map/ppermute | solution.py:253
  86.4 7.9 %collective-permute-start = (bf16[64,2048]{1,0:T(8,128)(2,1)}, bf16[64,2048]{1,0:T(8,128)(2,1)}, u32[]{:S(2)}, u32[]{:S(2)}) collective-permute-start(bf16[64,2048]{1,0:T(8,128)(2,1)} %own_ref.1), channel_id=1, source_target_pairs={{0,16},{1,17},{2,18},{3,19},{4,20},{5,21},{6,22},{7,23},{8,24},{9,... | collective-permute-start | bytes 786440 | tf_op jit(solution)/shard_map/ppermute | solution.py:244
  89.7 14.2 %copy-start.8 = (bf16[2,384,256]{2,1,0:T(8,128)(2,1)}, bf16[2,384,256]{2,1,0:T(8,128)(2,1)S(1)}, u32[]{:S(2)}) copy-start(bf16[2,384,256]{2,1,0:T(8,128)(2,1)S(1)} %collective-permute-done.7.refs_1_) | copy-start | bytes 1179652
  89.7 14.2 %collective-permute-start.8 = (bf16[2,384,256]{2,1,0:T(8,128)(2,1)S(1)}, bf16[2,384,256]{2,1,0:T(8,128)(2,1)}, u32[]{:S(2)}, u32[]{:S(2)}) collective-permute-start(bf16[2,384,256]{2,1,0:T(8,128)(2,1)S(1)} %collective-permute-done.7.refs_1_), channel_id=1, source_target_pairs={{0,1},{1,2},{2,3},{3,4},{4,5},{5,6},{6,7},{7,8},{8,9},{9,10},{10,1... | collective-permute-start | bytes 1179656 | tf_op jit(solution)/shard_map/ppermute | solution.py:253
  97.4 28.8 %collective-permute-start.16 = (bf16[2,384,256]{2,1,0:T(8,128)(2,1)}, bf16[2,384,256]{2,1,0:T(8,128)(2,1)}, u32[]{:S(2)}, u32[]{:S(2)}) collective-permute-start(bf16[2,384,256]{2,1,0:T(8,128)(2,1)} %collective-permute-done.15.refs_2_), channel_id=1, source_target_pairs={{0,15},{1,0},{2,1},{3,2},{4,3},{5,4},{6,5},{7,6},{8,7},{9,8},{10,9... | collective-permute-start | bytes 1179656 | tf_op jit(solution)/shard_map/ppermute | solution.py:253
  103.9 25.8 %collective-permute-start.9 = (bf16[2,384,256]{2,1,0:T(8,128)(2,1)}, bf16[2,384,256]{2,1,0:T(8,128)(2,1)S(1)}, u32[]{:S(2)}, u32[]{:S(2)}) collective-permute-start(bf16[2,384,256]{2,1,0:T(8,128)(2,1)} %collective-permute-done.8.refs_1_), channel_id=1, source_target_pairs={{0,1},{1,2},{2,3},{3,4},{4,5},{5,6},{6,7},{7,8},{8,9},{9,10},{10,1... | collective-permute-start | bytes 1179656 | tf_op jit(solution)/shard_map/ppermute | solution.py:253
  129.8 0.7 copy-start.9
  134.0 25.5 %collective-permute-start.17 = (bf16[384,256]{1,0:T(8,128)(2,1)}, bf16[384,256]{1,0:T(8,128)(2,1)S(1)}, u32[]{:S(2)}, u32[]{:S(2)}) collective-permute-start(bf16[384,256]{1,0:T(8,128)(2,1)} %get-tuple-element.14), channel_id=1, source_target_pairs={{0,16},{1,17},{2,18},{3,19},{4,20},{5,21},{6,22},{7,23},{8,24},{9,... | collective-permute-start | bytes 589832 | tf_op jit(solution)/shard_map/ppermute | solution.py:277
  137.1 22.5 %collective-permute-start.18 = (bf16[192,256]{1,0:T(8,128)(2,1)}, bf16[192,256]{1,0:T(8,128)(2,1)S(1)}, u32[]{:S(2)}, u32[]{:S(2)}) collective-permute-start(bf16[192,256]{1,0:T(8,128)(2,1)} %get-tuple-element.15), channel_id=1, source_target_pairs={{16,80},{64,0},{17,81},{65,1},{18,82},{66,2},{19,83},{67,3},{20,84... | collective-permute-start | bytes 294920 | tf_op jit(solution)/shard_map/ppermute | solution.py:278
  147.2 12.4 %collective-permute-start.19 = (bf16[192,256]{1,0:T(8,128)(2,1)}, bf16[192,256]{1,0:T(8,128)(2,1)S(1)}, u32[]{:S(2)}, u32[]{:S(2)}) collective-permute-start(bf16[192,256]{1,0:T(8,128)(2,1)} %get-tuple-element.16), channel_id=1, source_target_pairs={{16,64},{64,16},{17,65},{65,17},{18,66},{66,18},{19,67},{67,19},{2... | collective-permute-start | bytes 294920 | tf_op jit(solution)/shard_map/ppermute | solution.py:279
  149.1 8.5 %collective-permute-start.20 = (bf16[8,4,256]{2,1,0:T(4,128)(2,1)}, bf16[8,4,256]{2,1,0:T(4,128)(2,1)S(1)}, u32[]{:S(2)}, u32[]{:S(2)}) collective-permute-start(bf16[8,4,256]{2,1,0:T(4,128)(2,1)} %get-tuple-element.17), channel_id=1, source_target_pairs={{0,32},{32,0},{1,33},{33,1},{2,34},{34,2},{3,35},{35,3},{4,36},{36... | collective-permute-start | bytes 49160 | tf_op jit(solution)/shard_map/ppermute | solution.py:280
  153.6 5.9 %collective-permute-start.21 = (bf16[8,4,256]{2,1,0:T(4,128)(2,1)}, bf16[8,4,256]{2,1,0:T(4,128)(2,1)S(1)}, u32[]{:S(2)}, u32[]{:S(2)}) collective-permute-start(bf16[8,4,256]{2,1,0:T(4,128)(2,1)} %get-tuple-element.18), channel_id=1, source_target_pairs={{0,48},{1,49},{2,50},{3,51},{4,52},{5,53},{6,54},{7,55},{8,56},{9,... | collective-permute-start | bytes 49160 | tf_op jit(solution)/shard_map/ppermute | solution.py:286
  157.6 2.0 %copy-start.14 = (bf16[8,4,256]{2,1,0:T(4,128)(2,1)}, bf16[8,4,256]{2,1,0:T(4,128)(2,1)S(1)}, u32[]{:S(2)}) copy-start(bf16[8,4,256]{2,1,0:T(4,128)(2,1)S(1)} %collective-permute-done.20.keep_y_ref) | copy-start | bytes 49156
  159.5 0.6 copy-start.15
  159.5 0.7 copy-start.12
  159.5 0.7 copy-start.13
  159.6 0.7 copy-start.11
